TPU v7x, 256 devices: a whole 4x4x8 slice. The times are simulated.
256 devices in a mesh: site: 8 (over y, core), row: 32 (over z, x).
Axes of the slice: x: 4, y: 4, z: 8, core: 2. Of those that a mesh axis runs over, the one named last changes fastest.
Arguments:
- mps_cores: bfloat16 [8, 64, 4, 128, 128], P('site', None, None, 'row'), may hold values from -1 to 1
- live_sizes: int32 [8, 64], P('site', 'row'), may hold values from 32 to 128, as said below
- retained_sizes: int32 [8, 64], P('site', 'row'), may hold values from 32 to 128, as said below
- pattern: int32 [8, 64, 4], P('site', 'row'), may hold values from 0 to 1, as said below
Outputs:
- ortho_cores: float32 [8, 64, 4, 128, 128], P('site', None, None, 'row')
- bond_factor: float32 [8, 64, 128, 128], P('site', None, 'row')
Inputs may be any that keep to these rules, and one draw needn't show every extreme that they name: live_sizes[0, 0] = 128; for every core k and sector s, retained_sizes[k, s] <= live_sizes[k, s], and live_sizes[k + 1, s] <= retained_sizes[k, s]. retained_sizes[0, 0] = 128. pattern[k, s, 0] = 1 for every core k and sector s.
All inputs are finite; a program needn't handle non-finite values.
Results may differ from a plain program's by a relative error of at most 0.0003.
Values may be sent and summed in bfloat16 or wider, within the bound.
No kernel may reach another device: no remote copies, remote signals or barrier semaphores. Data moves between devices by JAX's collectives and lax.ppermute only.
A program may use at most 64 MiB of HBM per device.

v0:
```python
import functools
import math

import jax
import jax.numpy as jnp
from jax import lax
from jax.experimental import pallas as pl
from jax.experimental.pallas import tpu as pltpu
from jax.sharding import PartitionSpec as P

SB = 128
PANEL = 8
F32 = jnp.float32
BF16 = jnp.bfloat16
NN = (((1,), (0,)), ((), ()))
NT = (((1,), (1,)), ((), ()))
TN = (((0,), (0,)), ((), ()))
VMEM_BYTES = 24 * 1024 * 1024
VMEM_SPEC = pl.BlockSpec(memory_space=pltpu.VMEM)
SMEM_SPEC = pl.BlockSpec(memory_space=pltpu.SMEM)


def dot(a, b, dims):
    return lax.dot_general(a, b, dims, preferred_element_type=F32)


def split(x, parts):
    out = []
    for _ in range(parts):
        piece = x.astype(BF16)
        out.append(piece)
        x = x - piece.astype(F32)
    return out


HALF = SB // 2
SLABS = HALF // PANEL


def lanes(shape=(PANEL, SB)):
    return lax.broadcasted_iota(jnp.int32, shape, 1)


def rows_of(shape=(PANEL, SB)):
    return lax.broadcasted_iota(jnp.int32, shape, 0)


def row_spread(x, i):
    return jnp.broadcast_to(x[i : i + 1, :], (PANEL, SB))


def sweep(main, others, emit):
    lane, sub = lanes(), rows_of()
    high = jnp.where(lane >= HALF, HALF, 0)

    def spread(x, j):
        return jnp.take_along_axis(x, high + j, axis=1, mode="promise_in_bounds")

    tables = [list(main)] + [list(o) for o in others]
    for t in range(SLABS):
        base = PANEL * t
        cols = [spread(tables[0][t], base + i) for i in range(PANEL)]
        nxt = t + 1 if t + 1 < SLABS else None
        far = range(t + 2, SLABS)
        near = [spread(tables[0][nxt], base + i) for i in range(PANEL)] if nxt else None
        fc = {u: [spread(tables[0][u], base + i) for i in range(PANEL)] for u in far}
        diag = None
        ws = [[] for _ in tables]
        ls = {}
        for i in range(PANEL):
            c = cols[i]
            diag = c if i == 0 else jnp.where(sub == i, c, diag)
            inv = row_spread(1.0 / c, i)
            li = jnp.where(sub > i, c, 0.0) * inv
            for m in range(i + 1, PANEL):
                cols[m] = cols[m] - li * row_spread(cols[m], i)
                ls[m, i] = row_spread(li, m)
            for w, table in zip(ws, tables):
                row = row_spread(table[t], i)
                w.append(row * inv)
                if i < PANEL - 1:
                    table[t] = table[t] - li * row
                if nxt:
                    table[nxt] = table[nxt] - near[i] * w[i]
            if nxt:
                for m in range(i + 1, PANEL):
                    near[m] = near[m] - near[i] * ls[m, i]
        emit(t, tables[0][t], [table[t] for table in tables[1:]], diag)
        if not len(far):
            continue
        for z, table in zip(ws, tables):
            for i in range(PANEL - 2, -1, -1):
                for m in range(PANEL - 1, i, -1):
                    z[i] = z[i] - ls[m, i] * z[m]
            for u in far:
                total = fc[u][0] * z[0]
                for i in range(1, PANEL):
                    total = total + fc[u][i] * z[i]
                table[u] = table[u] - total


ORDER = ((0, 0), (1, 1), (1, 2), (1, 0), (0, 1), (0, 2), (1, 3), (0, 3))
GROUPS = (((0, 0), 0, 3), ((0, 1), 3, 1), ((1, 1), 4, 3), ((1, 0), 7, 1))
PACKET = (3 * HALF, SB)


def assembled(packet):
    left = lanes((HALF, SB)) < HALF
    u11, u12, u22 = (packet[HALF * k : HALF * (k + 1), :] for k in range(3))
    r11, r12, r22 = (pltpu.roll(u, HALF, 1) for u in (u11, u12, u22))
    first = jnp.concatenate([jnp.where(left, u11, r12), jnp.where(left, 0.0, r22)], axis=0)
    second = jnp.concatenate([jnp.where(left, r11, u12), jnp.where(left, 0.0, u22)], axis=0)
    return first, second


def factors(flags, own, low):
    shape = (SB, SB)
    eye = rows_of(shape) == lanes(shape)
    first = flags[1] == 1
    own_eye = jnp.where(eye, 1.0, 0.0)
    low_eye = jnp.where(eye & (flags[2] == 1), 1.0, 0.0)
    out = {}
    for which, value in enumerate(assembled(own)):
        out[0, which] = jnp.where(first, own_eye, value)
    for which, value in enumerate(assembled(low)):
        out[1, which] = jnp.where(first, low_eye, value)
    return out


def product(a, b, dims):
    total = dot(a[1], b[1], dims) + (dot(a[0], b[2], dims) + dot(a[2], b[0], dims))
    total = total + (dot(a[0], b[1], dims) + dot(a[1], b[0], dims))
    return total + dot(a[0], b[0], dims)


def halves(both):
    return jnp.where(lanes((HALF, SB)) < HALF, both[:HALF, :], both[HALF:, :])


def slabs_of(x):
    return [x[PANEL * t : PANEL * (t + 1), :] for t in range(SLABS)]


def grams(flags, parts_of, at_ref):
    blocks = {}
    for key, start, number in GROUPS:
        lhs = at_ref[start * SB : (start + number) * SB, :]
        total = None
        for piece in reversed(parts_of[key]):
            term = dot(lhs, piece, NT)
            total = term if total is None else total + term
        for k in range(number):
            blocks[ORDER[start + k]] = total[k * SB : (k + 1) * SB, :]
    tops = jnp.concatenate([jnp.concatenate([blocks[s, p][:HALF, :] for s in range(2)], axis=0) for p in range(4)], axis=1)
    lows = jnp.concatenate([jnp.concatenate([blocks[s, p][HALF:, :] for s in range(2)], axis=0) for p in range(4)], axis=1)
    tops, lows = split(tops, 3), split(lows, 3)
    both = [jnp.concatenate([a, b], axis=0) for a, b in zip(tops, lows)]
    upper = product(tops, both, NT)
    shape = (HALF, SB)
    live = jnp.where(lanes(shape) < HALF, flags[3], flags[4])
    row = rows_of(shape)
    same = row == (lanes(shape) & (HALF - 1))
    g11 = halves(upper[:, :SB]) + jnp.where(same & (row >= live), 1.0, 0.0)
    g22 = halves(product(lows, lows, NT)) + jnp.where(same & (row + HALF >= live), 1.0, 0.0)
    return g11, halves(upper[:, SB:]), g22


def factorize(flags, parts_of, at_ref, u_ref, w_ref):
    g11, g12, g22 = grams(flags, parts_of, at_ref)
    lane, sub = lanes(), rows_of()
    place = lane & (HALF - 1)
    kept = jnp.where(lane < HALF, flags[5], flags[6])
    scaling = math.sqrt(4 * SB)
    eye = [jnp.where(place == sub + PANEL * t, 1.0, 0.0) for t in range(SLABS)]
    u12, w11 = [], []

    def first(t, head, rest, diag):
        row = sub + PANEL * t
        root = lax.rsqrt(diag)
        at = slice(PANEL * t, PANEL * (t + 1))
        u12.append(rest[0] * root)
        u_ref[at, :] = jnp.where((place >= row) & (row < kept), head * root, 0.0)
        u_ref[slice(at.start + HALF, at.stop + HALF), :] = jnp.where(row < kept, u12[t], 0.0)
        if w_ref is not None:
            w11.append(rest[1] * root)
            w_ref[at, :] = jnp.where(row < kept, w11[t] * scaling, 0.0)

    sweep(slabs_of(g11), [slabs_of(g12)] + ([eye] if w_ref is not None else []), first)
    cross = split(jnp.concatenate(u12, axis=0), 3)
    others = []
    if w_ref is not None:
        below = halves(product(cross, split(jnp.concatenate(w11, axis=0), 3), TN))
        others = [slabs_of(-below), eye]

    def second(t, head, rest, diag):
        row = sub + PANEL * t
        stay = row + HALF < kept
        root = lax.rsqrt(diag)
        u_ref[2 * HALF + PANEL * t : 2 * HALF + PANEL * (t + 1), :] = jnp.where((place >= row) & stay, head * root, 0.0)
        for k, value in enumerate(rest):
            at = HALF * (k + 1) + PANEL * t
            w_ref[at : at + PANEL, :] = jnp.where(stay, value * (root * scaling), 0.0)

    sweep(slabs_of(g22 - halves(product(cross, cross, TN))), others, second)


def round_kernel(at, flags, own_ref, low_ref, at_ref, _, out_ref, state_ref):
    @pl.when(flags[0] == at)
    def _():
        own, low = own_ref[...], low_ref[...]
        state_ref[0], state_ref[1] = own, low
        found = factors(flags, own, low)
        factorize(flags, {k: split(v, 3) for k, v in found.items()}, at_ref, out_ref, None)


def last_kernel(at, flags, own_ref, low_ref, state_ref, at_ref, a_ref, out_ref, w_ref, u_ref):
    here = flags[0] == at
    own = jnp.where(here, own_ref[...], state_ref[0])
    low = jnp.where(here, low_ref[...], state_ref[1])
    found = factors(flags, own, low)
    factorize(flags, {k: split(v, 3) for k, v in found.items()}, at_ref, u_ref, w_ref)
    pair = {k: split(v, 2) for k, v in found.items()}
    met = {}
    for key, start, number in GROUPS:
        for k in range(number):
            met[ORDER[start + k]] = (key, start + k)
    left = lanes((HALF, SB)) < HALF
    w11, w21, w22 = (w_ref[HALF * k : HALF * (k + 1), :] for k in range(3))
    r11, r21, r22 = (pltpu.roll(w, HALF, 1) for w in (w11, w21, w22))
    inverse = (
        jnp.concatenate([jnp.where(left, w11, 0.0), jnp.where(left, w21, r22)], axis=0),
        jnp.concatenate([jnp.where(left, r11, 0.0), jnp.where(left, r21, w22)], axis=0),
    )
    factor = assembled(u_ref[...])
    for s in range(2):
        w_hi, w_lo = split(inverse[s], 2)
        for p in range(4):
            key, start = met[s, p]
            core = a_ref[start * SB : (start + 1) * SB, :]
            turned = dot(core, w_lo, NT) + dot(core, w_hi, NT)
            t_hi, t_lo = split(turned, 2)
            p_hi, p_lo = pair[key]
            block = (dot(p_lo, t_hi, NN) + dot(p_hi, t_lo, NN)) + dot(p_hi, t_hi, NN)
            out_ref[:, s * 16 + p * 4 : s * 16 + p * 4 + 4, :] = block.reshape(32, 4, SB)
        out_ref[:, 32 + 4 * s : 36 + 4 * s, :] = factor[s].reshape(32, 4, SB)


def shards(mps_cores, live_sizes, retained_sizes, pattern):
    n_site = lax.axis_size("site")
    n_row = lax.axis_size("row")
    site_at = lax.axis_index("site")
    row_at = lax.axis_index("row")
    sent = mps_cores.reshape(n_row, 32, SB)
    got = lax.all_to_all(sent, "row", split_axis=0, concat_axis=0, tiled=True)
    got = got.reshape(n_row, 2, 4, 4, SB)
    live, kept = live_sizes[0], retained_sizes[0]
    column = lax.broadcasted_iota(jnp.int32, (2, 4, SB), 2)
    mask = (column < live[:, None, None]) & (pattern[0][:, :, None] != 0)
    cores = jnp.transpose(got, (1, 2, 0, 3, 4)).reshape(2, 4, SB, SB)
    cores = jnp.where(mask[:, :, None, :], cores, jnp.zeros((), cores.dtype))
    stacked = jnp.stack([cores[s, p] for s, p in ORDER])
    a_all = stacked.reshape(8 * SB, SB)
    at_all = jnp.swapaxes(stacked, 1, 2).reshape(8 * SB, SB)
    head = jnp.stack([site_at, (site_at == 0).astype(jnp.int32), (row_at > 0).astype(jnp.int32)])
    flags = jnp.concatenate([head.astype(jnp.int32), live, kept])
    params = pltpu.CompilerParams(vmem_limit_bytes=VMEM_BYTES)
    packet = jax.ShapeDtypeStruct(PACKET, F32)
    own = low = jnp.zeros(PACKET, F32)
    state = jnp.zeros((2,) + PACKET, F32)
    for at in range(n_site - 1):
        factor, state = pl.pallas_call(
            functools.partial(round_kernel, at),
            out_shape=(packet, jax.ShapeDtypeStruct(state.shape, F32)),
            in_specs=[SMEM_SPEC] + [VMEM_SPEC] * 4,
            out_specs=(VMEM_SPEC, VMEM_SPEC),
            input_output_aliases={4: 1},
            compiler_params=params,
            name="round",
        )(flags, own, low, at_all, state)
        here, there = n_row * at, n_row * (at + 1)
        low = lax.ppermute(factor, ("site", "row"), [(here + i, there + i + 1) for i in range(n_row - 1)])
        own = lax.ppermute(factor, ("site", "row"), [(here + i, there + i) for i in range(n_row)])
    out = pl.pallas_call(
        functools.partial(last_kernel, n_site - 1),
        out_shape=jax.ShapeDtypeStruct((32, 40, SB), F32),
        in_specs=[SMEM_SPEC] + [VMEM_SPEC] * 5,
        out_specs=VMEM_SPEC,
        scratch_shapes=[pltpu.VMEM(PACKET, F32), pltpu.VMEM(PACKET, F32)],
        compiler_params=params,
        name="last",
    )(flags, own, low, state, at_all, a_all)
    back = lax.all_to_all(out, "row", split_axis=0, concat_axis=0, tiled=True)
    ortho = back[:, :32].reshape(1, 2 * n_row, 4, 4, SB)
    factor = back[:, 32:].reshape(1, 2 * n_row, 4, SB)
    return (ortho, factor)


def solution(mesh):
    in_specs = (
        P("site", None, None, "row", None),
        P("site", "row"),
        P("site", "row"),
        P("site", "row", None),
    )
    out_specs = (P("site", None, None, "row", None), P("site", None, "row", None))
    return jax.shard_map(shards, mesh=mesh, in_specs=in_specs, out_specs=out_specs, check_vma=False)
```

profile of v0, /device:TPU:25, one launch (start us, length us, event | category | flops | bytes accessed | tf_op | source)
XLA Modules:
  0.0 134.3 jit_solution(3494174055943921376)
XLA Ops:
  0.6 11.0 %all-to-all-start = ((bf16[32,32,128]{2,1,0:T(8,128)(2,1)}), bf16[32,32,128]{2,1,0:T(8,128)(2,1)S(1)}, u32[]{:S(2)}, u32[]{:S(2)}) async-start(bf16[32,32,128]{2,1,0:T(8,128)(2,1)} %bitcast.62), calls=%async_computation | async-start | bytes 524288 | tf_op jit(solution)/shard_map/all_to_all | solution.py:254
  11.7 0.0 copy-start
  11.7 0.0 copy-start.1
  11.7 0.6 copy-done
  12.4 0.0 copy-done.1
  12.4 0.1 concatenate.3.flags
  12.4 0.6 copy-done.2
  13.1 0.1 fusion.8
  13.1 9.9 %all-to-all-done = bf16[32,32,128]{2,1,0:T(8,128)(2,1)S(1)} async-done(((bf16[32,32,128]{2,1,0:T(8,128)(2,1)}), bf16[32,32,128]{2,1,0:T(8,128)(2,1)S(1)}, u32[]{:S(2)}, u32[]{:S(2)}) %all-to-all-start) | async-done | bytes 262176 | tf_op jit(solution)/shard_map/all_to_all | solution.py:254
  23.0 0.1 copy.13
  23.2 0.2 copy.14
  23.5 0.6 round.7
  24.0 0.7 collective-permute-start.1
  24.7 0.7 collective-permute-start
  25.4 0.0 collective-permute-done.1.low_ref
  25.4 0.0 collective-permute-done.own_ref
  25.4 0.6 round.8
  26.0 0.7 collective-permute-start.3
  26.6 0.7 collective-permute-start.2
  27.3 0.0 collective-permute-done.3.low_ref
  27.3 0.0 collective-permute-done.2.own_ref
  27.3 0.6 round.9
  27.9 0.7 collective-permute-start.5
  28.6 0.7 collective-permute-start.4
  29.2 0.0 collective-permute-done.5.low_ref
  29.2 0.0 collective-permute-done.4.own_ref
  29.3 0.7 round.10
  30.0 0.7 collective-permute-start.7
  30.7 0.7 collective-permute-start.6
  31.3 0.0 collective-permute-done.7.low_ref
  31.4 0.0 collective-permute-done.6.own_ref
  31.4 0.6 round.11
  31.9 0.7 collective-permute-start.9
  32.6 0.7 collective-permute-start.8
  33.3 0.0 collective-permute-done.9.low_ref
  33.3 0.0 collective-permute-done.8.own_ref
  33.3 0.6 round.12
  33.9 0.7 collective-permute-start.11
  34.5 0.7 collective-permute-start.10
  35.2 0.0 collective-permute-done.10.own_ref
  35.2 0.6 round.13
  35.8 0.7 collective-permute-start.13
  36.5 1.5 %collective-permute-start.12 = (f32[192,128]{1,0:T(8,128)S(1)}, f32[192,128]{1,0:T(8,128)S(1)}, u32[]{:S(2)}, u32[]{:S(2)}) collective-permute-start(f32[192,128]{1,0:T(8,128)S(1)} %get-tuple-element.28), channel_id=1, source_target_pairs={{192,224},{193,225},{194,226},{195,227},{196,228},{197,229},{198,2... | collective-permute-start | bytes 294920 | tf_op jit(solution)/shard_map/ppermute | solution.py:282
  38.0 56.4 %collective-permute-done.12.own_ref = f32[192,128]{1,0:T(8,128)S(1)} collective-permute-done((f32[192,128]{1,0:T(8,128)S(1)}, f32[192,128]{1,0:T(8,128)S(1)}, u32[]{:S(2)}, u32[]{:S(2)}) %collective-permute-start.12) | collective-permute-done | bytes 98336 | tf_op jit(solution)/shard_map/ppermute | solution.py:282
  94.3 7.1 %last.1 = f32[32,40,128]{2,1,0:T(8,128)S(1)} custom-call(s32[7]{0:T(128)S(1)} %concatenate.3.flags, f32[192,128]{1,0:T(8,128)S(1)} %collective-permute-done.12.own_ref, f32[192,128]{1,0:T(8,128)S(1)} %collective-permute-done.13.low_ref, f32[2,192,128]{2,1,0:T(8,128)S(1)} %get-tuple-element.29.state_ref, bf16[1024,128]{1,0:T(8,128)(2,1)S(1)} %bitcast.56, ...), custom_call_target="tpu_custom_call" | custom-call | tf_op jit(solution)/shard_map/last/pallas_call | solution.py:283
  101.4 31.4 %all_to_all.10 = f32[32,40,128]{2,1,0:T(8,128)S(1)} all-to-all(f32[32,40,128]{2,1,0:T(8,128)S(1)} %last.1), channel_id=1, replica_groups=mesh['site'=8,'row'=32] {'row'}, dimensions={0} | all-to-all | bytes 1310720 | tf_op jit(solution)/shard_map/all_to_all | solution.py:292
  132.8 0.7 slice.49
  133.5 0.9 slice.48
  (15 shorter events, 0.1 us)
Async XLA Ops:
  0.6 22.4 %all-to-all-start = ((bf16[32,32,128]{2,1,0:T(8,128)(2,1)}), bf16[32,32,128]{2,1,0:T(8,128)(2,1)S(1)}, u32[]{:S(2)}, u32[]{:S(2)}) async-start(bf16[32,32,128]{2,1,0:T(8,128)(2,1)} %bitcast.62), calls=%async_computation | async-start | bytes 524288 | tf_op jit(solution)/shard_map/all_to_all | solution.py:254
  11.7 0.7 copy-start
  11.7 0.7 copy-start.1
  12.4 0.7 copy-start.2
  24.0 1.4 %collective-permute-start.1 = (f32[192,128]{1,0:T(8,128)S(1)}, f32[192,128]{1,0:T(8,128)S(1)}, u32[]{:S(2)}, u32[]{:S(2)}) collective-permute-start(f32[192,128]{1,0:T(8,128)S(1)} %get-tuple-element.16), channel_id=1, source_target_pairs={{0,33},{1,34},{2,35},{3,36},{4,37},{5,38},{6,39},{7,40},{8,41},{9,... | collective-permute-start | bytes 294920 | tf_op jit(solution)/shard_map/ppermute | solution.py:281
  24.7 0.7 collective-permute-start
  26.0 1.4 %collective-permute-start.3 = (f32[192,128]{1,0:T(8,128)S(1)}, f32[192,128]{1,0:T(8,128)S(1)}, u32[]{:S(2)}, u32[]{:S(2)}) collective-permute-start(f32[192,128]{1,0:T(8,128)S(1)} %get-tuple-element.18), channel_id=1, source_target_pairs={{32,65},{33,66},{34,67},{35,68},{36,69},{37,70},{38,71},{39,72},{4... | collective-permute-start | bytes 294920 | tf_op jit(solution)/shard_map/ppermute | solution.py:281
  26.6 0.7 collective-permute-start.2
  27.9 1.4 %collective-permute-start.5 = (f32[192,128]{1,0:T(8,128)S(1)}, f32[192,128]{1,0:T(8,128)S(1)}, u32[]{:S(2)}, u32[]{:S(2)}) collective-permute-start(f32[192,128]{1,0:T(8,128)S(1)} %get-tuple-element.20), channel_id=1, source_target_pairs={{64,97},{65,98},{66,99},{67,100},{68,101},{69,102},{70,103},{71,10... | collective-permute-start | bytes 294920 | tf_op jit(solution)/shard_map/ppermute | solution.py:281
  28.6 0.7 collective-permute-start.4
  30.0 1.4 %collective-permute-start.7 = (f32[192,128]{1,0:T(8,128)S(1)}, f32[192,128]{1,0:T(8,128)S(1)}, u32[]{:S(2)}, u32[]{:S(2)}) collective-permute-start(f32[192,128]{1,0:T(8,128)S(1)} %get-tuple-element.22), channel_id=1, source_target_pairs={{96,129},{97,130},{98,131},{99,132},{100,133},{101,134},{102,135},... | collective-permute-start | bytes 294920 | tf_op jit(solution)/shard_map/ppermute | solution.py:281
  30.7 0.7 collective-permute-start.6
  31.9 1.4 %collective-permute-start.9 = (f32[192,128]{1,0:T(8,128)S(1)}, f32[192,128]{1,0:T(8,128)S(1)}, u32[]{:S(2)}, u32[]{:S(2)}) collective-permute-start(f32[192,128]{1,0:T(8,128)S(1)} %get-tuple-element.24), channel_id=1, source_target_pairs={{128,161},{129,162},{130,163},{131,164},{132,165},{133,166},{134,1... | collective-permute-start | bytes 294920 | tf_op jit(solution)/shard_map/ppermute | solution.py:281
  32.6 0.7 collective-permute-start.8
  33.9 1.4 %collective-permute-start.11 = (f32[192,128]{1,0:T(8,128)S(1)}, f32[192,128]{1,0:T(8,128)S(1)}, u32[]{:S(2)}, u32[]{:S(2)}) collective-permute-start(f32[192,128]{1,0:T(8,128)S(1)} %get-tuple-element.26), channel_id=1, source_target_pairs={{160,193},{161,194},{162,195},{163,196},{164,197},{165,198},{166,1... | collective-permute-start | bytes 294920 | tf_op jit(solution)/shard_map/ppermute | solution.py:281
  34.5 0.7 collective-permute-start.10
  35.8 2.2 %collective-permute-start.13 = (f32[192,128]{1,0:T(8,128)S(1)}, f32[192,128]{1,0:T(8,128)S(1)}, u32[]{:S(2)}, u32[]{:S(2)}) collective-permute-start(f32[192,128]{1,0:T(8,128)S(1)} %get-tuple-element.28), channel_id=1, source_target_pairs={{192,225},{193,226},{194,227},{195,228},{196,229},{197,230},{198,2... | collective-permute-start | bytes 294920 | tf_op jit(solution)/shard_map/ppermute | solution.py:281
  36.5 57.9 %collective-permute-start.12 = (f32[192,128]{1,0:T(8,128)S(1)}, f32[192,128]{1,0:T(8,128)S(1)}, u32[]{:S(2)}, u32[]{:S(2)}) collective-permute-start(f32[192,128]{1,0:T(8,128)S(1)} %get-tuple-element.28), channel_id=1, source_target_pairs={{192,224},{193,225},{194,226},{195,227},{196,228},{197,229},{198,2... | collective-permute-start | bytes 294920 | tf_op jit(solution)/shard_map/ppermute | solution.py:282
where the time goes:
time: 135 us; the launch traced here: 134 us
  waiting for transfers between devices  66.3 us (49%)
  blocking collectives  31.4 us (23%)
  starting transfers between devices  21.2 us (16%)
  Pallas kernels  11.1 us (8%)
  local copies, waits for them, and re-layouts  3.23 us (2%)
    ppermute x7, waiting for transfers between devices, shards(): lax.ppermute(factor, ('site', 'row'), [(here + i, there + i) for i in ran...  56.4 us
    all_to_all x1, blocking collectives, shards(): back = lax.all_to_all(out, 'row', split_axis=0, concat_axis=0, tiled=True)  31.4 us
    all_to_all x1, starting transfers between devices, shards(): got = lax.all_to_all(sent, 'row', split_axis=0, concat_axis=0, tiled=True)  11 us
    all_to_all x1, waiting for transfers between devices, shards(): got = lax.all_to_all(sent, 'row', split_axis=0, concat_axis=0, tiled=True)  9.86 us
    pallas_call x1, Pallas kernels, shards(): pl.pallas_call(functools.partial(last_kernel, n_site - 1), out_shape=jax....  7.08 us
    ppermute x7, starting transfers between devices, shards(): lax.ppermute(factor, ('site', 'row'), [(here + i, there + i) for i in ran...  5.51 us
    ppermute x7, starting transfers between devices, shards(): lax.ppermute(factor, ('site', 'row'), [(here + i, there + i + 1) for i in...  4.67 us
    pallas_call x7, Pallas kernels, shards(): pl.pallas_call(functools.partial(round_kernel, at), out_shape=(packet, ja...  4.03 us
  transfers between devices with their start and end apart: 15, of which 2 were waited for; matrix products, arithmetic and copies ran while one was open for 0% of the time, Pallas kernels for 0%

commit v1 on v0

--- a/solution.py
+++ b/solution.py
@@ -59,10 +59,12 @@
     tables = [list(main)] + [list(o) for o in others]
     for t in range(SLABS):
         base = PANEL * t
-        cols = [spread(tables[0][t], base + i) for i in range(PANEL)]
+        cols = [spread(tables[0][t], i) for i in range(PANEL)] if t == 0 else ahead
         nxt = t + 1 if t + 1 < SLABS else None
-        far = range(t + 2, SLABS)
-        near = [spread(tables[0][nxt], base + i) for i in range(PANEL)] if nxt else None
+        ahead = [spread(tables[0][nxt], base + PANEL + i) for i in range(PANEL)] if nxt else None
+        close = range(t + 1, min(t + 2 + 1, SLABS))
+        far = range(t + 2 + 1, SLABS)
+        near = {u: [spread(tables[0][u], base + i) for i in range(PANEL)] for u in close}
         fc = {u: [spread(tables[0][u], base + i) for i in range(PANEL)] for u in far}
         diag = None
         ws = [[] for _ in tables]
@@ -80,11 +82,15 @@
                 w.append(row * inv)
                 if i < PANEL - 1:
                     table[t] = table[t] - li * row
-                if nxt:
-                    table[nxt] = table[nxt] - near[i] * w[i]
+                for u in close:
+                    table[u] = table[u] - near[u][i] * w[i]
+            for u in close:
+                for m in range(i + 1, PANEL):
+                    near[u][m] = near[u][m] - near[u][i] * ls[m, i]
             if nxt:
-                for m in range(i + 1, PANEL):
-                    near[m] = near[m] - near[i] * ls[m, i]
+                part = near[nxt][i] * inv
+                for m in range(PANEL):
+                    ahead[m] = ahead[m] - near[nxt][i] * row_spread(part, m)
         emit(t, tables[0][t], [table[t] for table in tables[1:]], diag)
         if not len(far):
             continue
@@ -128,9 +134,10 @@
 
 
 def product(a, b, dims):
-    total = dot(a[1], b[1], dims) + (dot(a[0], b[2], dims) + dot(a[2], b[0], dims))
-    total = total + (dot(a[0], b[1], dims) + dot(a[1], b[0], dims))
-    return total + dot(a[0], b[0], dims)
+    axes = dims[0][0][0], dims[0][1][0]
+    left = jnp.concatenate([a[k] for k in (1, 0, 2, 0, 1, 0)], axis=axes[0])
+    right = jnp.concatenate([b[k] for k in (1, 2, 0, 1, 0, 0)], axis=axes[1])
+    return dot(left, right, dims)
 
 
 def halves(both):
@@ -145,10 +152,8 @@
     blocks = {}
     for key, start, number in GROUPS:
         lhs = at_ref[start * SB : (start + number) * SB, :]
-        total = None
-        for piece in reversed(parts_of[key]):
-            term = dot(lhs, piece, NT)
-            total = term if total is None else total + term
+        pieces = parts_of[key]
+        total = dot(jnp.concatenate([lhs] * len(pieces), axis=1), jnp.concatenate(pieces[::-1], axis=1), NT)
         for k in range(number):
             blocks[ORDER[start + k]] = total[k * SB : (k + 1) * SB, :]
     tops = jnp.concatenate([jnp.concatenate([blocks[s, p][:HALF, :] for s in range(2)], axis=0) for p in range(4)], axis=1)

time: 135 us -> 127 us (0.941)
  waiting for transfers between devices: 66.3 us -> 59.2 us
    ppermute x7, waiting for transfers between devices: 56.4 us -> 49.3 us  [shards(): lax.ppermute(factor, ('site', 'row'), [(here + i, there + i) for i in ran...]
where the time goes in v1:
time: 127 us
  waiting for transfers between devices  59.2 us (47%)
  blocking collectives  31.4 us (25%)
  starting transfers between devices  21 us (17%)
  Pallas kernels  10.7 us (8%)
  local copies, waits for them, and re-layouts  3.23 us (3%)
    ppermute x7, waiting for transfers between devices, shards(): lax.ppermute(factor, ('site', 'row'), [(here + i, there + i) for i in ran...  49.3 us
    all_to_all x1, blocking collectives, shards(): back = lax.all_to_all(out, 'row', split_axis=0, concat_axis=0, tiled=True)  31.4 us
    all_to_all x1, starting transfers between devices, shards(): got = lax.all_to_all(sent, 'row', split_axis=0, concat_axis=0, tiled=True)  11 us
    all_to_all x1, waiting for transfers between devices, shards(): got = lax.all_to_all(sent, 'row', split_axis=0, concat_axis=0, tiled=True)  9.86 us
    pallas_call x1, Pallas kernels, shards(): pl.pallas_call(functools.partial(last_kernel, n_site - 1), out_shape=jax....  6.42 us
    ppermute x7, starting transfers between devices, shards(): lax.ppermute(factor, ('site', 'row'), [(here + i, there + i) for i in ran...  5.29 us
    ppermute x7, starting transfers between devices, shards(): lax.ppermute(factor, ('site', 'row'), [(here + i, there + i + 1) for i in...  4.67 us
    pallas_call x7, Pallas kernels, shards(): pl.pallas_call(functools.partial(round_kernel, at), out_shape=(packet, ja...  4.25 us
  transfers between devices with their start and end apart: 15, of which 2 were waited for; matrix products, arithmetic and copies ran while one was open for 0% of the time, Pallas kernels for 0%

profile of v1, /device:TPU:25, one launch (start us, length us, event | category | flops | bytes accessed | tf_op | source)
XLA Modules:
  0.0 126.6 jit_solution(11013189035339188540)
XLA Ops:
  0.6 11.0 %all-to-all-start = ((bf16[32,32,128]{2,1,0:T(8,128)(2,1)}), bf16[32,32,128]{2,1,0:T(8,128)(2,1)S(1)}, u32[]{:S(2)}, u32[]{:S(2)}) async-start(bf16[32,32,128]{2,1,0:T(8,128)(2,1)} %bitcast.62), calls=%async_computation | async-start | bytes 524288 | tf_op jit(solution)/shard_map/all_to_all | solution.py:259
  11.7 0.0 copy-start
  11.7 0.0 copy-start.1
  11.7 0.6 copy-done
  12.4 0.0 copy-done.1
  12.4 0.1 concatenate.3.flags
  12.4 0.6 copy-done.2
  13.1 0.1 fusion.8
  13.1 9.9 %all-to-all-done = bf16[32,32,128]{2,1,0:T(8,128)(2,1)S(1)} async-done(((bf16[32,32,128]{2,1,0:T(8,128)(2,1)}), bf16[32,32,128]{2,1,0:T(8,128)(2,1)S(1)}, u32[]{:S(2)}, u32[]{:S(2)}) %all-to-all-start) | async-done | bytes 262176 | tf_op jit(solution)/shard_map/all_to_all | solution.py:259
  23.0 0.1 copy.13
  23.2 0.2 copy.14
  23.5 0.6 round.7
  24.0 0.7 collective-permute-start.1
  24.7 0.7 collective-permute-start
  25.4 0.0 collective-permute-done.1.low_ref
  25.4 0.0 collective-permute-done.own_ref
  25.4 0.6 round.8
  26.0 0.7 collective-permute-start.3
  26.6 0.7 collective-permute-start.2
  27.3 0.0 collective-permute-done.3.low_ref
  27.3 0.0 collective-permute-done.2.own_ref
  27.3 0.6 round.9
  27.9 0.7 collective-permute-start.5
  28.6 0.7 collective-permute-start.4
  29.2 0.0 collective-permute-done.5.low_ref
  29.2 0.0 collective-permute-done.4.own_ref
  29.3 0.7 round.10
  30.0 0.7 collective-permute-start.7
  30.7 0.7 collective-permute-start.6
  31.3 0.0 collective-permute-done.7.low_ref
  31.4 0.0 collective-permute-done.6.own_ref
  31.4 0.6 round.11
  31.9 0.7 collective-permute-start.9
  32.6 0.7 collective-permute-start.8
  33.3 0.0 collective-permute-done.8.own_ref
  33.3 0.6 round.12
  33.9 0.7 collective-permute-start.11
  34.5 0.7 collective-permute-start.10
  35.2 0.0 collective-permute-done.11.low_ref
  35.2 0.0 collective-permute-done.10.own_ref
  35.2 0.8 round.13
  36.0 0.7 collective-permute-start.13
  36.7 1.3 %collective-permute-start.12 = (f32[192,128]{1,0:T(8,128)S(1)}, f32[192,128]{1,0:T(8,128)S(1)}, u32[]{:S(2)}, u32[]{:S(2)}) collective-permute-start(f32[192,128]{1,0:T(8,128)S(1)} %get-tuple-element.28), channel_id=1, source_target_pairs={{192,224},{193,225},{194,226},{195,227},{196,228},{197,229},{198,2... | collective-permute-start | bytes 294920 | tf_op jit(solution)/shard_map/ppermute | solution.py:287
  38.0 49.3 %collective-permute-done.12.own_ref = f32[192,128]{1,0:T(8,128)S(1)} collective-permute-done((f32[192,128]{1,0:T(8,128)S(1)}, f32[192,128]{1,0:T(8,128)S(1)}, u32[]{:S(2)}, u32[]{:S(2)}) %collective-permute-start.12) | collective-permute-done | bytes 98336 | tf_op jit(solution)/shard_map/ppermute | solution.py:287
  87.3 6.4 %last.1 = f32[32,40,128]{2,1,0:T(8,128)S(1)} custom-call(s32[7]{0:T(128)S(1)} %concatenate.3.flags, f32[192,128]{1,0:T(8,128)S(1)} %collective-permute-done.12.own_ref, f32[192,128]{1,0:T(8,128)S(1)} %collective-permute-done.13.low_ref, f32[2,192,128]{2,1,0:T(8,128)S(1)} %get-tuple-element.29.state_ref, bf16[1024,128]{1,0:T(8,128)(2,1)S(1)} %bitcast.56, ...), custom_call_target="tpu_custom_call" | custom-call | tf_op jit(solution)/shard_map/last/pallas_call | solution.py:288
  93.7 31.4 %all_to_all.10 = f32[32,40,128]{2,1,0:T(8,128)S(1)} all-to-all(f32[32,40,128]{2,1,0:T(8,128)S(1)} %last.1), channel_id=1, replica_groups=mesh['site'=8,'row'=32] {'row'}, dimensions={0} | all-to-all | bytes 1310720 | tf_op jit(solution)/shard_map/all_to_all | solution.py:297
  125.0 0.7 slice.49
  125.7 0.9 slice.48
  (15 shorter events, 0.1 us)
Async XLA Ops:
  0.6 22.4 %all-to-all-start = ((bf16[32,32,128]{2,1,0:T(8,128)(2,1)}), bf16[32,32,128]{2,1,0:T(8,128)(2,1)S(1)}, u32[]{:S(2)}, u32[]{:S(2)}) async-start(bf16[32,32,128]{2,1,0:T(8,128)(2,1)} %bitcast.62), calls=%async_computation | async-start | bytes 524288 | tf_op jit(solution)/shard_map/all_to_all | solution.py:259
  11.7 0.7 copy-start
  11.7 0.7 copy-start.1
  12.4 0.7 copy-start.2
  24.0 1.4 %collective-permute-start.1 = (f32[192,128]{1,0:T(8,128)S(1)}, f32[192,128]{1,0:T(8,128)S(1)}, u32[]{:S(2)}, u32[]{:S(2)}) collective-permute-start(f32[192,128]{1,0:T(8,128)S(1)} %get-tuple-element.16), channel_id=1, source_target_pairs={{0,33},{1,34},{2,35},{3,36},{4,37},{5,38},{6,39},{7,40},{8,41},{9,... | collective-permute-start | bytes 294920 | tf_op jit(solution)/shard_map/ppermute | solution.py:286
  24.7 0.7 collective-permute-start
  26.0 1.4 %collective-permute-start.3 = (f32[192,128]{1,0:T(8,128)S(1)}, f32[192,128]{1,0:T(8,128)S(1)}, u32[]{:S(2)}, u32[]{:S(2)}) collective-permute-start(f32[192,128]{1,0:T(8,128)S(1)} %get-tuple-element.18), channel_id=1, source_target_pairs={{32,65},{33,66},{34,67},{35,68},{36,69},{37,70},{38,71},{39,72},{4... | collective-permute-start | bytes 294920 | tf_op jit(solution)/shard_map/ppermute | solution.py:286
  26.6 0.7 collective-permute-start.2
  27.9 1.4 %collective-permute-start.5 = (f32[192,128]{1,0:T(8,128)S(1)}, f32[192,128]{1,0:T(8,128)S(1)}, u32[]{:S(2)}, u32[]{:S(2)}) collective-permute-start(f32[192,128]{1,0:T(8,128)S(1)} %get-tuple-element.20), channel_id=1, source_target_pairs={{64,97},{65,98},{66,99},{67,100},{68,101},{69,102},{70,103},{71,10... | collective-permute-start | bytes 294920 | tf_op jit(solution)/shard_map/ppermute | solution.py:286
  28.6 0.7 collective-permute-start.4
  30.0 1.4 %collective-permute-start.7 = (f32[192,128]{1,0:T(8,128)S(1)}, f32[192,128]{1,0:T(8,128)S(1)}, u32[]{:S(2)}, u32[]{:S(2)}) collective-permute-start(f32[192,128]{1,0:T(8,128)S(1)} %get-tuple-element.22), channel_id=1, source_target_pairs={{96,129},{97,130},{98,131},{99,132},{100,133},{101,134},{102,135},... | collective-permute-start | bytes 294920 | tf_op jit(solution)/shard_map/ppermute | solution.py:286
  30.7 0.7 collective-permute-start.6
  31.9 1.4 %collective-permute-start.9 = (f32[192,128]{1,0:T(8,128)S(1)}, f32[192,128]{1,0:T(8,128)S(1)}, u32[]{:S(2)}, u32[]{:S(2)}) collective-permute-start(f32[192,128]{1,0:T(8,128)S(1)} %get-tuple-element.24), channel_id=1, source_target_pairs={{128,161},{129,162},{130,163},{131,164},{132,165},{133,166},{134,1... | collective-permute-start | bytes 294920 | tf_op jit(solution)/shard_map/ppermute | solution.py:286
  32.6 0.7 collective-permute-start.8
  33.9 1.4 %collective-permute-start.11 = (f32[192,128]{1,0:T(8,128)S(1)}, f32[192,128]{1,0:T(8,128)S(1)}, u32[]{:S(2)}, u32[]{:S(2)}) collective-permute-start(f32[192,128]{1,0:T(8,128)S(1)} %get-tuple-element.26), channel_id=1, source_target_pairs={{160,193},{161,194},{162,195},{163,196},{164,197},{165,198},{166,1... | collective-permute-start | bytes 294920 | tf_op jit(solution)/shard_map/ppermute | solution.py:286
  34.5 0.7 collective-permute-start.10
  36.0 2.0 %collective-permute-start.13 = (f32[192,128]{1,0:T(8,128)S(1)}, f32[192,128]{1,0:T(8,128)S(1)}, u32[]{:S(2)}, u32[]{:S(2)}) collective-permute-start(f32[192,128]{1,0:T(8,128)S(1)} %get-tuple-element.28), channel_id=1, source_target_pairs={{192,225},{193,226},{194,227},{195,228},{196,229},{197,230},{198,2... | collective-permute-start | bytes 294920 | tf_op jit(solution)/shard_map/ppermute | solution.py:286
  36.7 50.6 %collective-permute-start.12 = (f32[192,128]{1,0:T(8,128)S(1)}, f32[192,128]{1,0:T(8,128)S(1)}, u32[]{:S(2)}, u32[]{:S(2)}) collective-permute-start(f32[192,128]{1,0:T(8,128)S(1)} %get-tuple-element.28), channel_id=1, source_target_pairs={{192,224},{193,225},{194,226},{195,227},{196,228},{197,229},{198,2... | collective-permute-start | bytes 294920 | tf_op jit(solution)/shard_map/ppermute | solution.py:287

commit v2 on v1

--- a/solution.py
+++ b/solution.py
@@ -135,8 +135,8 @@
 
 def product(a, b, dims):
     axes = dims[0][0][0], dims[0][1][0]
-    left = jnp.concatenate([a[k] for k in (1, 0, 2, 0, 1, 0)], axis=axes[0])
-    right = jnp.concatenate([b[k] for k in (1, 2, 0, 1, 0, 0)], axis=axes[1])
+    left = jnp.concatenate([a[k] for k in (1, 0, 0)], axis=axes[0])
+    right = jnp.concatenate([b[k] for k in (0, 1, 0)], axis=axes[1])
     return dot(left, right, dims)
 
 
@@ -158,7 +158,7 @@
             blocks[ORDER[start + k]] = total[k * SB : (k + 1) * SB, :]
     tops = jnp.concatenate([jnp.concatenate([blocks[s, p][:HALF, :] for s in range(2)], axis=0) for p in range(4)], axis=1)
     lows = jnp.concatenate([jnp.concatenate([blocks[s, p][HALF:, :] for s in range(2)], axis=0) for p in range(4)], axis=1)
-    tops, lows = split(tops, 3), split(lows, 3)
+    tops, lows = split(tops, 2), split(lows, 2)
     both = [jnp.concatenate([a, b], axis=0) for a, b in zip(tops, lows)]
     upper = product(tops, both, NT)
     shape = (HALF, SB)
@@ -191,10 +191,10 @@
             w_ref[at, :] = jnp.where(row < kept, w11[t] * scaling, 0.0)
 
     sweep(slabs_of(g11), [slabs_of(g12)] + ([eye] if w_ref is not None else []), first)
-    cross = split(jnp.concatenate(u12, axis=0), 3)
+    cross = split(jnp.concatenate(u12, axis=0), 2)
     others = []
     if w_ref is not None:
-        below = halves(product(cross, split(jnp.concatenate(w11, axis=0), 3), TN))
+        below = halves(product(cross, split(jnp.concatenate(w11, axis=0), 2), TN))
         others = [slabs_of(-below), eye]
 
     def second(t, head, rest, diag):
@@ -209,22 +209,22 @@
     sweep(slabs_of(g22 - halves(product(cross, cross, TN))), others, second)
 
 
-def round_kernel(at, flags, own_ref, low_ref, at_ref, _, out_ref, state_ref):
+def round_kernel(at, flags, low_ref, own_ref, at_ref, _, out_ref, state_ref):
     @pl.when(flags[0] == at)
     def _():
         own, low = own_ref[...], low_ref[...]
         state_ref[0], state_ref[1] = own, low
         found = factors(flags, own, low)
-        factorize(flags, {k: split(v, 3) for k, v in found.items()}, at_ref, out_ref, None)
-
-
-def last_kernel(at, flags, own_ref, low_ref, state_ref, at_ref, a_ref, out_ref, w_ref, u_ref):
+        factorize(flags, {k: split(v, 2) for k, v in found.items()}, at_ref, out_ref, None)
+
+
+def last_kernel(at, flags, low_ref, own_ref, state_ref, at_ref, a_ref, out_ref, w_ref, u_ref):
     here = flags[0] == at
     own = jnp.where(here, own_ref[...], state_ref[0])
     low = jnp.where(here, low_ref[...], state_ref[1])
     found = factors(flags, own, low)
-    factorize(flags, {k: split(v, 3) for k, v in found.items()}, at_ref, u_ref, w_ref)
     pair = {k: split(v, 2) for k, v in found.items()}
+    factorize(flags, pair, at_ref, u_ref, w_ref)
     met = {}
     for key, start, number in GROUPS:
         for k in range(number):
@@ -281,10 +281,10 @@
             input_output_aliases={4: 1},
             compiler_params=params,
             name="round",
-        )(flags, own, low, at_all, state)
+        )(flags, low, own, at_all, state)
         here, there = n_row * at, n_row * (at + 1)
+        own = lax.ppermute(factor, ("site", "row"), [(here + i, there + i) for i in range(n_row)])
         low = lax.ppermute(factor, ("site", "row"), [(here + i, there + i + 1) for i in range(n_row - 1)])
-        own = lax.ppermute(factor, ("site", "row"), [(here + i, there + i) for i in range(n_row)])
     out = pl.pallas_call(
         functools.partial(last_kernel, n_site - 1),
         out_shape=jax.ShapeDtypeStruct((32, 40, SB), F32),
@@ -293,7 +293,7 @@
         scratch_shapes=[pltpu.VMEM(PACKET, F32), pltpu.VMEM(PACKET, F32)],
         compiler_params=params,
         name="last",
-    )(flags, own, low, state, at_all, a_all)
+    )(flags, low, own, state, at_all, a_all)
     back = lax.all_to_all(out, "row", split_axis=0, concat_axis=0, tiled=True)
     ortho = back[:, :32].reshape(1, 2 * n_row, 4, 4, SB)
     factor = back[:, 32:].reshape(1, 2 * n_row, 4, SB)

time: 127 us -> 129 us (1.016)
  blocking collectives: 31.4 us -> 46.6 us
  waiting for transfers between devices: 59.2 us -> 46.5 us
    all_to_all x1, blocking collectives: 31.4 us -> 46.6 us  [shards(): back = lax.all_to_all(out, 'row', split_axis=0, concat_axis=0, tiled=True)]
    ppermute x7, waiting for transfers between devices: 49.3 us -> 36.6 us  [shards(): lax.ppermute(factor, ('site', 'row'), [(here + i, there + i) for i in ran...]
where the time goes in v2:
time: 129 us; the launch traced here: 128 us
  blocking collectives  46.6 us (36%)
  waiting for transfers between devices  46.5 us (36%)
  starting transfers between devices  21.2 us (16%)
  Pallas kernels  9.84 us (8%)
  local copies, waits for them, and re-layouts  3.23 us (3%)
    all_to_all x1, blocking collectives, shards(): back = lax.all_to_all(out, 'row', split_axis=0, concat_axis=0, tiled=True)  46.6 us
    ppermute x7, waiting for transfers between devices, shards(): lax.ppermute(factor, ('site', 'row'), [(here + i, there + i) for i in ran...  36.6 us
    all_to_all x1, starting transfers between devices, shards(): got = lax.all_to_all(sent, 'row', split_axis=0, concat_axis=0, tiled=True)  11 us
    all_to_all x1, waiting for transfers between devices, shards(): got = lax.all_to_all(sent, 'row', split_axis=0, concat_axis=0, tiled=True)  9.86 us
    pallas_call x1, Pallas kernels, shards(): pl.pallas_call(functools.partial(last_kernel, n_site - 1), out_shape=jax....  5.99 us
    ppermute x7, starting transfers between devices, shards(): lax.ppermute(factor, ('site', 'row'), [(here + i, there + i) for i in ran...  5.29 us
    ppermute x7, starting transfers between devices, shards(): lax.ppermute(factor, ('site', 'row'), [(here + i, there + i + 1) for i in...  4.85 us
    pallas_call x7, Pallas kernels, shards(): pl.pallas_call(functools.partial(round_kernel, at), out_shape=(packet, ja...  3.85 us
  transfers between devices with their start and end apart: 15, of which 2 were waited for; matrix products, arithmetic and copies ran while one was open for 0% of the time, Pallas kernels for 0%

profile of v2, /device:TPU:25, one launch (start us, length us, event | category | flops | bytes accessed | tf_op | source)
XLA Modules:
  0.0 128.5 jit_solution(11887895907367955214)
XLA Ops:
  0.6 11.0 %all-to-all-start = ((bf16[32,32,128]{2,1,0:T(8,128)(2,1)}), bf16[32,32,128]{2,1,0:T(8,128)(2,1)S(1)}, u32[]{:S(2)}, u32[]{:S(2)}) async-start(bf16[32,32,128]{2,1,0:T(8,128)(2,1)} %bitcast.62), calls=%async_computation | async-start | bytes 524288 | tf_op jit(solution)/shard_map/all_to_all | solution.py:259
  11.7 0.0 copy-start
  11.7 0.0 copy-start.1
  11.7 0.6 copy-done
  12.4 0.0 copy-done.1
  12.4 0.1 concatenate.3.flags
  12.4 0.6 copy-done.2
  13.1 0.1 fusion.8
  13.1 9.9 %all-to-all-done = bf16[32,32,128]{2,1,0:T(8,128)(2,1)S(1)} async-done(((bf16[32,32,128]{2,1,0:T(8,128)(2,1)}), bf16[32,32,128]{2,1,0:T(8,128)(2,1)S(1)}, u32[]{:S(2)}, u32[]{:S(2)}) %all-to-all-start) | async-done | bytes 262176 | tf_op jit(solution)/shard_map/all_to_all | solution.py:259
  23.0 0.1 copy.13
  23.2 0.2 copy.14
  23.5 0.6 round.7
  24.0 0.7 collective-permute-start.1
  24.7 0.7 collective-permute-start
  25.4 0.0 collective-permute-done.1.own_ref
  25.4 0.0 collective-permute-done.low_ref
  25.4 0.6 round.8
  26.0 0.7 collective-permute-start.3
  26.6 0.7 collective-permute-start.2
  27.3 0.0 collective-permute-done.3.own_ref
  27.3 0.0 collective-permute-done.2.low_ref
  27.3 0.6 round.9
  27.9 0.7 collective-permute-start.5
  28.6 0.7 collective-permute-start.4
  29.2 0.0 collective-permute-done.5.own_ref
  29.2 0.0 collective-permute-done.4.low_ref
  29.3 0.6 round.10
  29.8 0.7 collective-permute-start.7
  30.5 0.8 collective-permute-start.6
  31.3 0.0 collective-permute-done.7.own_ref
  31.4 0.0 collective-permute-done.6.low_ref
  31.4 0.6 round.11
  31.9 0.7 collective-permute-start.9
  32.6 0.7 collective-permute-start.8
  33.3 0.0 collective-permute-done.9.own_ref
  33.3 0.0 collective-permute-done.8.low_ref
  33.3 0.6 round.12
  33.9 0.7 collective-permute-start.11
  34.5 0.7 collective-permute-start.10
  35.2 0.0 collective-permute-done.10.low_ref
  35.2 0.6 round.13
  35.8 1.3 %collective-permute-start.13 = (f32[192,128]{1,0:T(8,128)S(1)}, f32[192,128]{1,0:T(8,128)S(1)}, u32[]{:S(2)}, u32[]{:S(2)}) collective-permute-start(f32[192,128]{1,0:T(8,128)S(1)} %get-tuple-element.28), channel_id=1, source_target_pairs={{192,224},{193,225},{194,226},{195,227},{196,228},{197,229},{198,2... | collective-permute-start | bytes 294920 | tf_op jit(solution)/shard_map/ppermute | solution.py:286
  37.1 0.7 collective-permute-start.12
  37.8 36.6 %collective-permute-done.13.own_ref = f32[192,128]{1,0:T(8,128)S(1)} collective-permute-done((f32[192,128]{1,0:T(8,128)S(1)}, f32[192,128]{1,0:T(8,128)S(1)}, u32[]{:S(2)}, u32[]{:S(2)}) %collective-permute-start.13) | collective-permute-done | bytes 98336 | tf_op jit(solution)/shard_map/ppermute | solution.py:286
  74.4 6.0 %last.1 = f32[32,40,128]{2,1,0:T(8,128)S(1)} custom-call(s32[7]{0:T(128)S(1)} %concatenate.3.flags, f32[192,128]{1,0:T(8,128)S(1)} %collective-permute-done.12.low_ref, f32[192,128]{1,0:T(8,128)S(1)} %collective-permute-done.13.own_ref, f32[2,192,128]{2,1,0:T(8,128)S(1)} %get-tuple-element.29.state_ref, bf16[1024,128]{1,0:T(8,128)(2,1)S(1)} %bitcast.56, ...), custom_call_target="tpu_custom_call" | custom-call | tf_op jit(solution)/shard_map/last/pallas_call | solution.py:288
  80.4 46.6 %all_to_all.10 = f32[32,40,128]{2,1,0:T(8,128)S(1)} all-to-all(f32[32,40,128]{2,1,0:T(8,128)S(1)} %last.1), channel_id=1, replica_groups=mesh['site'=8,'row'=32] {'row'}, dimensions={0} | all-to-all | bytes 1310720 | tf_op jit(solution)/shard_map/all_to_all | solution.py:297
  127.0 0.7 slice.49
  127.6 0.9 slice.48
  (15 shorter events, 0.1 us)
Async XLA Ops:
  0.6 22.4 %all-to-all-start = ((bf16[32,32,128]{2,1,0:T(8,128)(2,1)}), bf16[32,32,128]{2,1,0:T(8,128)(2,1)S(1)}, u32[]{:S(2)}, u32[]{:S(2)}) async-start(bf16[32,32,128]{2,1,0:T(8,128)(2,1)} %bitcast.62), calls=%async_computation | async-start | bytes 524288 | tf_op jit(solution)/shard_map/all_to_all | solution.py:259
  11.7 0.7 copy-start
  11.7 0.7 copy-start.1
  12.4 0.7 copy-start.2
  24.0 1.4 %collective-permute-start.1 = (f32[192,128]{1,0:T(8,128)S(1)}, f32[192,128]{1,0:T(8,128)S(1)}, u32[]{:S(2)}, u32[]{:S(2)}) collective-permute-start(f32[192,128]{1,0:T(8,128)S(1)} %get-tuple-element.16), channel_id=1, source_target_pairs={{0,32},{1,33},{2,34},{3,35},{4,36},{5,37},{6,38},{7,39},{8,40},{9,... | collective-permute-start | bytes 294920 | tf_op jit(solution)/shard_map/ppermute | solution.py:286
  24.7 0.7 collective-permute-start
  26.0 1.4 %collective-permute-start.3 = (f32[192,128]{1,0:T(8,128)S(1)}, f32[192,128]{1,0:T(8,128)S(1)}, u32[]{:S(2)}, u32[]{:S(2)}) collective-permute-start(f32[192,128]{1,0:T(8,128)S(1)} %get-tuple-element.18), channel_id=1, source_target_pairs={{32,64},{33,65},{34,66},{35,67},{36,68},{37,69},{38,70},{39,71},{4... | collective-permute-start | bytes 294920 | tf_op jit(solution)/shard_map/ppermute | solution.py:286
  26.6 0.7 collective-permute-start.2
  27.9 1.4 %collective-permute-start.5 = (f32[192,128]{1,0:T(8,128)S(1)}, f32[192,128]{1,0:T(8,128)S(1)}, u32[]{:S(2)}, u32[]{:S(2)}) collective-permute-start(f32[192,128]{1,0:T(8,128)S(1)} %get-tuple-element.20), channel_id=1, source_target_pairs={{64,96},{65,97},{66,98},{67,99},{68,100},{69,101},{70,102},{71,103... | collective-permute-start | bytes 294920 | tf_op jit(solution)/shard_map/ppermute | solution.py:286
  28.6 0.7 collective-permute-start.4
  29.8 1.5 %collective-permute-start.7 = (f32[192,128]{1,0:T(8,128)S(1)}, f32[192,128]{1,0:T(8,128)S(1)}, u32[]{:S(2)}, u32[]{:S(2)}) collective-permute-start(f32[192,128]{1,0:T(8,128)S(1)} %get-tuple-element.22), channel_id=1, source_target_pairs={{96,128},{97,129},{98,130},{99,131},{100,132},{101,133},{102,134},... | collective-permute-start | bytes 294920 | tf_op jit(solution)/shard_map/ppermute | solution.py:286
  30.5 0.9 collective-permute-start.6
  31.9 1.4 %collective-permute-start.9 = (f32[192,128]{1,0:T(8,128)S(1)}, f32[192,128]{1,0:T(8,128)S(1)}, u32[]{:S(2)}, u32[]{:S(2)}) collective-permute-start(f32[192,128]{1,0:T(8,128)S(1)} %get-tuple-element.24), channel_id=1, source_target_pairs={{128,160},{129,161},{130,162},{131,163},{132,164},{133,165},{134,1... | collective-permute-start | bytes 294920 | tf_op jit(solution)/shard_map/ppermute | solution.py:286
  32.6 0.7 collective-permute-start.8
  33.9 1.4 %collective-permute-start.11 = (f32[192,128]{1,0:T(8,128)S(1)}, f32[192,128]{1,0:T(8,128)S(1)}, u32[]{:S(2)}, u32[]{:S(2)}) collective-permute-start(f32[192,128]{1,0:T(8,128)S(1)} %get-tuple-element.26), channel_id=1, source_target_pairs={{160,192},{161,193},{162,194},{163,195},{164,196},{165,197},{166,1... | collective-permute-start | bytes 294920 | tf_op jit(solution)/shard_map/ppermute | solution.py:286
  34.5 0.7 collective-permute-start.10
  35.8 38.6 %collective-permute-start.13 = (f32[192,128]{1,0:T(8,128)S(1)}, f32[192,128]{1,0:T(8,128)S(1)}, u32[]{:S(2)}, u32[]{:S(2)}) collective-permute-start(f32[192,128]{1,0:T(8,128)S(1)} %get-tuple-element.28), channel_id=1, source_target_pairs={{192,224},{193,225},{194,226},{195,227},{196,228},{197,229},{198,2... | collective-permute-start | bytes 294920 | tf_op jit(solution)/shard_map/ppermute | solution.py:286
  37.1 37.3 %collective-permute-start.12 = (f32[192,128]{1,0:T(8,128)S(1)}, f32[192,128]{1,0:T(8,128)S(1)}, u32[]{:S(2)}, u32[]{:S(2)}) collective-permute-start(f32[192,128]{1,0:T(8,128)S(1)} %get-tuple-element.28), channel_id=1, source_target_pairs={{192,225},{193,226},{194,227},{195,228},{196,229},{197,230},{198,2... | collective-permute-start | bytes 294920 | tf_op jit(solution)/shard_map/ppermute | solution.py:287

commit v3 on v2

--- a/solution.py
+++ b/solution.py
@@ -209,7 +209,7 @@
     sweep(slabs_of(g22 - halves(product(cross, cross, TN))), others, second)
 
 
-def round_kernel(at, flags, low_ref, own_ref, at_ref, _, out_ref, state_ref):
+def round_kernel(at, flags, own_ref, low_ref, at_ref, _, out_ref, state_ref):
     @pl.when(flags[0] == at)
     def _():
         own, low = own_ref[...], low_ref[...]
@@ -218,7 +218,7 @@
         factorize(flags, {k: split(v, 2) for k, v in found.items()}, at_ref, out_ref, None)
 
 
-def last_kernel(at, flags, low_ref, own_ref, state_ref, at_ref, a_ref, out_ref, w_ref, u_ref):
+def last_kernel(at, flags, own_ref, low_ref, state_ref, at_ref, a_ref, out_ref, w_ref, u_ref):
     here = flags[0] == at
     own = jnp.where(here, own_ref[...], state_ref[0])
     low = jnp.where(here, low_ref[...], state_ref[1])
@@ -281,7 +281,7 @@
             input_output_aliases={4: 1},
             compiler_params=params,
             name="round",
-        )(flags, low, own, at_all, state)
+        )(flags, own, low, at_all, state)
         here, there = n_row * at, n_row * (at + 1)
         own = lax.ppermute(factor, ("site", "row"), [(here + i, there + i) for i in range(n_row)])
         low = lax.ppermute(factor, ("site", "row"), [(here + i, there + i + 1) for i in range(n_row - 1)])
@@ -293,7 +293,7 @@
         scratch_shapes=[pltpu.VMEM(PACKET, F32), pltpu.VMEM(PACKET, F32)],
         compiler_params=params,
         name="last",
-    )(flags, low, own, state, at_all, a_all)
+    )(flags, own, low, state, at_all, a_all)
     back = lax.all_to_all(out, "row", split_axis=0, concat_axis=0, tiled=True)
     ortho = back[:, :32].reshape(1, 2 * n_row, 4, 4, SB)
     factor = back[:, 32:].reshape(1, 2 * n_row, 4, SB)

time: 129 us -> 123 us (0.953)
  blocking collectives: 46.6 us -> 31.2 us
  waiting for transfers between devices: 46.5 us -> 55.8 us
    all_to_all x1, blocking collectives: 46.6 us -> 31.2 us  [shards(): back = lax.all_to_all(out, 'row', split_axis=0, concat_axis=0, tiled=True)]
    ppermute x7, waiting for transfers between devices: 36.6 us -> 45.9 us  [shards(): lax.ppermute(factor, ('site', 'row'), [(here + i, there + i) for i in ran...]
where the time goes in v3:
time: 123 us; the launch traced here: 122 us
  waiting for transfers between devices  55.8 us (45%)
  blocking collectives  31.2 us (25%)
  starting transfers between devices  21.2 us (17%)
  Pallas kernels  9.84 us (8%)
  local copies, waits for them, and re-layouts  3.23 us (3%)
    ppermute x7, waiting for transfers between devices, shards(): lax.ppermute(factor, ('site', 'row'), [(here + i, there + i) for i in ran...  45.9 us
    all_to_all x1, blocking collectives, shards(): back = lax.all_to_all(out, 'row', split_axis=0, concat_axis=0, tiled=True)  31.2 us
    all_to_all x1, starting transfers between devices, shards(): got = lax.all_to_all(sent, 'row', split_axis=0, concat_axis=0, tiled=True)  11 us
    all_to_all x1, waiting for transfers between devices, shards(): got = lax.all_to_all(sent, 'row', split_axis=0, concat_axis=0, tiled=True)  9.86 us
    pallas_call x1, Pallas kernels, shards(): pl.pallas_call(functools.partial(last_kernel, n_site - 1), out_shape=jax....  5.98 us
    ppermute x7, starting transfers between devices, shards(): lax.ppermute(factor, ('site', 'row'), [(here + i, there + i) for i in ran...  5.47 us
    ppermute x7, starting transfers between devices, shards(): lax.ppermute(factor, ('site', 'row'), [(here + i, there + i + 1) for i in...  4.67 us
    pallas_call x7, Pallas kernels, shards(): pl.pallas_call(functools.partial(round_kernel, at), out_shape=(packet, ja...  3.85 us
  transfers between devices with their start and end apart: 15, of which 2 were waited for; matrix products, arithmetic and copies ran while one was open for 0% of the time, Pallas kernels for 0%

profile of v3, /device:TPU:25, one launch (start us, length us, event | category | flops | bytes accessed | tf_op | source)
XLA Modules:
  0.0 122.4 jit_solution(7536663664922327716)
XLA Ops:
  0.6 11.0 %all-to-all-start = ((bf16[32,32,128]{2,1,0:T(8,128)(2,1)}), bf16[32,32,128]{2,1,0:T(8,128)(2,1)S(1)}, u32[]{:S(2)}, u32[]{:S(2)}) async-start(bf16[32,32,128]{2,1,0:T(8,128)(2,1)} %bitcast.62), calls=%async_computation | async-start | bytes 524288 | tf_op jit(solution)/shard_map/all_to_all | solution.py:259
  11.7 0.0 copy-start
  11.7 0.0 copy-start.1
  11.7 0.6 copy-done
  12.4 0.0 copy-done.1
  12.4 0.1 concatenate.3.flags
  12.4 0.6 copy-done.2
  13.1 0.1 fusion.8
  13.1 9.9 %all-to-all-done = bf16[32,32,128]{2,1,0:T(8,128)(2,1)S(1)} async-done(((bf16[32,32,128]{2,1,0:T(8,128)(2,1)}), bf16[32,32,128]{2,1,0:T(8,128)(2,1)S(1)}, u32[]{:S(2)}, u32[]{:S(2)}) %all-to-all-start) | async-done | bytes 262176 | tf_op jit(solution)/shard_map/all_to_all | solution.py:259
  23.0 0.1 copy.13
  23.2 0.2 copy.14
  23.5 0.6 round.7
  24.0 0.7 collective-permute-start.1
  24.7 0.7 collective-permute-start
  25.4 0.0 collective-permute-done.1.low_ref
  25.4 0.0 collective-permute-done.own_ref
  25.4 0.6 round.8
  26.0 0.7 collective-permute-start.3
  26.6 0.7 collective-permute-start.2
  27.3 0.0 collective-permute-done.3.low_ref
  27.3 0.0 collective-permute-done.2.own_ref
  27.3 0.6 round.9
  27.9 0.7 collective-permute-start.5
  28.6 0.7 collective-permute-start.4
  29.2 0.0 collective-permute-done.5.low_ref
  29.2 0.0 collective-permute-done.4.own_ref
  29.3 0.6 round.10
  29.8 0.7 collective-permute-start.7
  30.5 0.8 collective-permute-start.6
  31.3 0.0 collective-permute-done.7.low_ref
  31.4 0.0 collective-permute-done.6.own_ref
  31.4 0.6 round.11
  31.9 0.7 collective-permute-start.9
  32.6 0.7 collective-permute-start.8
  33.3 0.0 collective-permute-done.9.low_ref
  33.3 0.0 collective-permute-done.8.own_ref
  33.3 0.6 round.12
  33.9 0.7 collective-permute-start.11
  34.5 0.7 collective-permute-start.10
  35.2 0.0 collective-permute-done.11.low_ref
  35.2 0.6 round.13
  35.8 0.7 collective-permute-start.13
  36.5 1.3 %collective-permute-start.12 = (f32[192,128]{1,0:T(8,128)S(1)}, f32[192,128]{1,0:T(8,128)S(1)}, u32[]{:S(2)}, u32[]{:S(2)}) collective-permute-start(f32[192,128]{1,0:T(8,128)S(1)} %get-tuple-element.28), channel_id=1, source_target_pairs={{192,224},{193,225},{194,226},{195,227},{196,228},{197,229},{198,2... | collective-permute-start | bytes 294920 | tf_op jit(solution)/shard_map/ppermute | solution.py:286
  37.8 45.9 %collective-permute-done.12.own_ref = f32[192,128]{1,0:T(8,128)S(1)} collective-permute-done((f32[192,128]{1,0:T(8,128)S(1)}, f32[192,128]{1,0:T(8,128)S(1)}, u32[]{:S(2)}, u32[]{:S(2)}) %collective-permute-start.12) | collective-permute-done | bytes 98336 | tf_op jit(solution)/shard_map/ppermute | solution.py:286
  83.7 6.0 %last.1 = f32[32,40,128]{2,1,0:T(8,128)S(1)} custom-call(s32[7]{0:T(128)S(1)} %concatenate.3.flags, f32[192,128]{1,0:T(8,128)S(1)} %collective-permute-done.12.own_ref, f32[192,128]{1,0:T(8,128)S(1)} %collective-permute-done.13.low_ref, f32[2,192,128]{2,1,0:T(8,128)S(1)} %get-tuple-element.29.state_ref, bf16[1024,128]{1,0:T(8,128)(2,1)S(1)} %bitcast.56, ...), custom_call_target="tpu_custom_call" | custom-call | tf_op jit(solution)/shard_map/last/pallas_call | solution.py:288
  89.7 31.2 %all_to_all.10 = f32[32,40,128]{2,1,0:T(8,128)S(1)} all-to-all(f32[32,40,128]{2,1,0:T(8,128)S(1)} %last.1), channel_id=1, replica_groups=mesh['site'=8,'row'=32] {'row'}, dimensions={0} | all-to-all | bytes 1310720 | tf_op jit(solution)/shard_map/all_to_all | solution.py:297
  120.8 0.7 slice.49
  121.5 0.9 slice.48
  (15 shorter events, 0.1 us)
Async XLA Ops:
  0.6 22.4 %all-to-all-start = ((bf16[32,32,128]{2,1,0:T(8,128)(2,1)}), bf16[32,32,128]{2,1,0:T(8,128)(2,1)S(1)}, u32[]{:S(2)}, u32[]{:S(2)}) async-start(bf16[32,32,128]{2,1,0:T(8,128)(2,1)} %bitcast.62), calls=%async_computation | async-start | bytes 524288 | tf_op jit(solution)/shard_map/all_to_all | solution.py:259
  11.7 0.7 copy-start
  11.7 0.7 copy-start.1
  12.4 0.7 copy-start.2
  24.0 1.4 %collective-permute-start.1 = (f32[192,128]{1,0:T(8,128)S(1)}, f32[192,128]{1,0:T(8,128)S(1)}, u32[]{:S(2)}, u32[]{:S(2)}) collective-permute-start(f32[192,128]{1,0:T(8,128)S(1)} %get-tuple-element.16), channel_id=1, source_target_pairs={{0,33},{1,34},{2,35},{3,36},{4,37},{5,38},{6,39},{7,40},{8,41},{9,... | collective-permute-start | bytes 294920 | tf_op jit(solution)/shard_map/ppermute | solution.py:287
  24.7 0.7 collective-permute-start
  26.0 1.4 %collective-permute-start.3 = (f32[192,128]{1,0:T(8,128)S(1)}, f32[192,128]{1,0:T(8,128)S(1)}, u32[]{:S(2)}, u32[]{:S(2)}) collective-permute-start(f32[192,128]{1,0:T(8,128)S(1)} %get-tuple-element.18), channel_id=1, source_target_pairs={{32,65},{33,66},{34,67},{35,68},{36,69},{37,70},{38,71},{39,72},{4... | collective-permute-start | bytes 294920 | tf_op jit(solution)/shard_map/ppermute | solution.py:287
  26.6 0.7 collective-permute-start.2
  27.9 1.4 %collective-permute-start.5 = (f32[192,128]{1,0:T(8,128)S(1)}, f32[192,128]{1,0:T(8,128)S(1)}, u32[]{:S(2)}, u32[]{:S(2)}) collective-permute-start(f32[192,128]{1,0:T(8,128)S(1)} %get-tuple-element.20), channel_id=1, source_target_pairs={{64,97},{65,98},{66,99},{67,100},{68,101},{69,102},{70,103},{71,10... | collective-permute-start | bytes 294920 | tf_op jit(solution)/shard_map/ppermute | solution.py:287
  28.6 0.7 collective-permute-start.4
  29.8 1.5 %collective-permute-start.7 = (f32[192,128]{1,0:T(8,128)S(1)}, f32[192,128]{1,0:T(8,128)S(1)}, u32[]{:S(2)}, u32[]{:S(2)}) collective-permute-start(f32[192,128]{1,0:T(8,128)S(1)} %get-tuple-element.22), channel_id=1, source_target_pairs={{96,129},{97,130},{98,131},{99,132},{100,133},{101,134},{102,135},... | collective-permute-start | bytes 294920 | tf_op jit(solution)/shard_map/ppermute | solution.py:287
  30.5 0.9 collective-permute-start.6
  31.9 1.4 %collective-permute-start.9 = (f32[192,128]{1,0:T(8,128)S(1)}, f32[192,128]{1,0:T(8,128)S(1)}, u32[]{:S(2)}, u32[]{:S(2)}) collective-permute-start(f32[192,128]{1,0:T(8,128)S(1)} %get-tuple-element.24), channel_id=1, source_target_pairs={{128,161},{129,162},{130,163},{131,164},{132,165},{133,166},{134,1... | collective-permute-start | bytes 294920 | tf_op jit(solution)/shard_map/ppermute | solution.py:287
  32.6 0.7 collective-permute-start.8
  33.9 1.4 %collective-permute-start.11 = (f32[192,128]{1,0:T(8,128)S(1)}, f32[192,128]{1,0:T(8,128)S(1)}, u32[]{:S(2)}, u32[]{:S(2)}) collective-permute-start(f32[192,128]{1,0:T(8,128)S(1)} %get-tuple-element.26), channel_id=1, source_target_pairs={{160,193},{161,194},{162,195},{163,196},{164,197},{165,198},{166,1... | collective-permute-start | bytes 294920 | tf_op jit(solution)/shard_map/ppermute | solution.py:287
  34.5 0.7 collective-permute-start.10
  35.8 2.0 %collective-permute-start.13 = (f32[192,128]{1,0:T(8,128)S(1)}, f32[192,128]{1,0:T(8,128)S(1)}, u32[]{:S(2)}, u32[]{:S(2)}) collective-permute-start(f32[192,128]{1,0:T(8,128)S(1)} %get-tuple-element.28), channel_id=1, source_target_pairs={{192,225},{193,226},{194,227},{195,228},{196,229},{197,230},{198,2... | collective-permute-start | bytes 294920 | tf_op jit(solution)/shard_map/ppermute | solution.py:287
  36.5 47.2 %collective-permute-start.12 = (f32[192,128]{1,0:T(8,128)S(1)}, f32[192,128]{1,0:T(8,128)S(1)}, u32[]{:S(2)}, u32[]{:S(2)}) collective-permute-start(f32[192,128]{1,0:T(8,128)S(1)} %get-tuple-element.28), channel_id=1, source_target_pairs={{192,224},{193,225},{194,226},{195,227},{196,228},{197,229},{198,2... | collective-permute-start | bytes 294920 | tf_op jit(solution)/shard_map/ppermute | solution.py:286

commit v4 on v3

--- a/solution.py
+++ b/solution.py
@@ -238,14 +238,13 @@
     )
     factor = assembled(u_ref[...])
     for s in range(2):
+        cores = jnp.concatenate([a_ref[met[s, p][1] * SB : (met[s, p][1] + 1) * SB, :] for p in range(4)], axis=0)
         w_hi, w_lo = split(inverse[s], 2)
+        turned = dot(jnp.concatenate([cores, cores], axis=1), jnp.concatenate([w_lo, w_hi], axis=1), NT)
+        t_hi, t_lo = split(turned, 2)
         for p in range(4):
-            key, start = met[s, p]
-            core = a_ref[start * SB : (start + 1) * SB, :]
-            turned = dot(core, w_lo, NT) + dot(core, w_hi, NT)
-            t_hi, t_lo = split(turned, 2)
-            p_hi, p_lo = pair[key]
-            block = (dot(p_lo, t_hi, NN) + dot(p_hi, t_lo, NN)) + dot(p_hi, t_hi, NN)
+            at = slice(p * SB, (p + 1) * SB)
+            block = product(pair[met[s, p][0]], [t_hi[at, :], t_lo[at, :]], NN)
             out_ref[:, s * 16 + p * 4 : s * 16 + p * 4 + 4, :] = block.reshape(32, 4, SB)
         out_ref[:, 32 + 4 * s : 36 + 4 * s, :] = factor[s].reshape(32, 4, SB)
 

time: 123 us -> 122 us (level)
  no operation moved by 1% of the time
where the time goes in v4:
time: 122 us; the launch traced here: 121 us
  waiting for transfers between devices  55.8 us (46%)
  blocking collectives  31.2 us (26%)
  starting transfers between devices  21.2 us (17%)
  Pallas kernels  8.73 us (7%)
  local copies, waits for them, and re-layouts  3.23 us (3%)
    ppermute x7, waiting for transfers between devices, shards(): lax.ppermute(factor, ('site', 'row'), [(here + i, there + i) for i in ran...  45.9 us
    all_to_all x1, blocking collectives, shards(): back = lax.all_to_all(out, 'row', split_axis=0, concat_axis=0, tiled=True)  31.2 us
    all_to_all x1, starting transfers between devices, shards(): got = lax.all_to_all(sent, 'row', split_axis=0, concat_axis=0, tiled=True)  11 us
    all_to_all x1, waiting for transfers between devices, shards(): got = lax.all_to_all(sent, 'row', split_axis=0, concat_axis=0, tiled=True)  9.86 us
    ppermute x7, starting transfers between devices, shards(): lax.ppermute(factor, ('site', 'row'), [(here + i, there + i) for i in ran...  5.47 us
    pallas_call x1, Pallas kernels, shards(): pl.pallas_call(functools.partial(last_kernel, n_site - 1), out_shape=jax....  4.88 us
    ppermute x7, starting transfers between devices, shards(): lax.ppermute(factor, ('site', 'row'), [(here + i, there + i + 1) for i in...  4.67 us
    pallas_call x7, Pallas kernels, shards(): pl.pallas_call(functools.partial(round_kernel, at), out_shape=(packet, ja...  3.85 us
  transfers between devices with their start and end apart: 15, of which 2 were waited for; matrix products, arithmetic and copies ran while one was open for 0% of the time, Pallas kernels for 0%

profile of v4, /device:TPU:25, one launch (start us, length us, event | category | flops | bytes accessed | tf_op | source)
XLA Modules:
  0.0 121.2 jit_solution(16370796345470929269)
XLA Ops:
  0.6 11.0 %all-to-all-start = ((bf16[32,32,128]{2,1,0:T(8,128)(2,1)}), bf16[32,32,128]{2,1,0:T(8,128)(2,1)S(1)}, u32[]{:S(2)}, u32[]{:S(2)}) async-start(bf16[32,32,128]{2,1,0:T(8,128)(2,1)} %bitcast.62), calls=%async_computation | async-start | bytes 524288 | tf_op jit(solution)/shard_map/all_to_all | solution.py:258
  11.7 0.0 copy-start
  11.7 0.0 copy-start.1
  11.7 0.6 copy-done
  12.4 0.0 copy-done.1
  12.4 0.1 concatenate.3.flags
  12.4 0.6 copy-done.2
  13.1 0.1 fusion.8
  13.1 9.9 %all-to-all-done = bf16[32,32,128]{2,1,0:T(8,128)(2,1)S(1)} async-done(((bf16[32,32,128]{2,1,0:T(8,128)(2,1)}), bf16[32,32,128]{2,1,0:T(8,128)(2,1)S(1)}, u32[]{:S(2)}, u32[]{:S(2)}) %all-to-all-start) | async-done | bytes 262176 | tf_op jit(solution)/shard_map/all_to_all | solution.py:258
  23.0 0.1 copy.13
  23.2 0.2 copy.14
  23.5 0.6 round.7
  24.0 0.7 collective-permute-start.1
  24.7 0.7 collective-permute-start
  25.4 0.0 collective-permute-done.1.low_ref
  25.4 0.0 collective-permute-done.own_ref
  25.4 0.6 round.8
  26.0 0.7 collective-permute-start.3
  26.6 0.7 collective-permute-start.2
  27.3 0.0 collective-permute-done.3.low_ref
  27.3 0.0 collective-permute-done.2.own_ref
  27.3 0.6 round.9
  27.9 0.7 collective-permute-start.5
  28.6 0.7 collective-permute-start.4
  29.2 0.0 collective-permute-done.5.low_ref
  29.2 0.0 collective-permute-done.4.own_ref
  29.3 0.6 round.10
  29.8 0.7 collective-permute-start.7
  30.5 0.8 collective-permute-start.6
  31.3 0.0 collective-permute-done.7.low_ref
  31.4 0.0 collective-permute-done.6.own_ref
  31.4 0.6 round.11
  31.9 0.7 collective-permute-start.9
  32.6 0.7 collective-permute-start.8
  33.3 0.0 collective-permute-done.9.low_ref
  33.3 0.6 round.12
  33.9 0.7 collective-permute-start.11
  34.5 0.7 collective-permute-start.10
  35.2 0.0 collective-permute-done.10.own_ref
  35.2 0.6 round.13
  35.8 0.7 collective-permute-start.13
  36.5 1.3 %collective-permute-start.12 = (f32[192,128]{1,0:T(8,128)S(1)}, f32[192,128]{1,0:T(8,128)S(1)}, u32[]{:S(2)}, u32[]{:S(2)}) collective-permute-start(f32[192,128]{1,0:T(8,128)S(1)} %get-tuple-element.28), channel_id=1, source_target_pairs={{192,224},{193,225},{194,226},{195,227},{196,228},{197,229},{198,2... | collective-permute-start | bytes 294920 | tf_op jit(solution)/shard_map/ppermute | solution.py:285
  37.8 0.0 collective-permute-done.13.low_ref
  37.8 45.9 %collective-permute-done.12.own_ref = f32[192,128]{1,0:T(8,128)S(1)} collective-permute-done((f32[192,128]{1,0:T(8,128)S(1)}, f32[192,128]{1,0:T(8,128)S(1)}, u32[]{:S(2)}, u32[]{:S(2)}) %collective-permute-start.12) | collective-permute-done | bytes 98336 | tf_op jit(solution)/shard_map/ppermute | solution.py:285
  83.7 4.9 %last.1 = f32[32,40,128]{2,1,0:T(8,128)S(1)} custom-call(s32[7]{0:T(128)S(1)} %concatenate.3.flags, f32[192,128]{1,0:T(8,128)S(1)} %collective-permute-done.12.own_ref, f32[192,128]{1,0:T(8,128)S(1)} %collective-permute-done.13.low_ref, f32[2,192,128]{2,1,0:T(8,128)S(1)} %get-tuple-element.29.state_ref, bf16[1024,128]{1,0:T(8,128)(2,1)S(1)} %bitcast.56, ...), custom_call_target="tpu_custom_call" | custom-call | tf_op jit(solution)/shard_map/last/pallas_call | solution.py:287
  88.5 31.2 %all_to_all.10 = f32[32,40,128]{2,1,0:T(8,128)S(1)} all-to-all(f32[32,40,128]{2,1,0:T(8,128)S(1)} %last.1), channel_id=1, replica_groups=mesh['site'=8,'row'=32] {'row'}, dimensions={0} | all-to-all | bytes 1310720 | tf_op jit(solution)/shard_map/all_to_all | solution.py:296
  119.7 0.7 slice.49
  120.4 0.9 slice.48
  (15 shorter events, 0.1 us)
Async XLA Ops:
  0.6 22.4 %all-to-all-start = ((bf16[32,32,128]{2,1,0:T(8,128)(2,1)}), bf16[32,32,128]{2,1,0:T(8,128)(2,1)S(1)}, u32[]{:S(2)}, u32[]{:S(2)}) async-start(bf16[32,32,128]{2,1,0:T(8,128)(2,1)} %bitcast.62), calls=%async_computation | async-start | bytes 524288 | tf_op jit(solution)/shard_map/all_to_all | solution.py:258
  11.7 0.7 copy-start
  11.7 0.7 copy-start.1
  12.4 0.7 copy-start.2
  24.0 1.4 %collective-permute-start.1 = (f32[192,128]{1,0:T(8,128)S(1)}, f32[192,128]{1,0:T(8,128)S(1)}, u32[]{:S(2)}, u32[]{:S(2)}) collective-permute-start(f32[192,128]{1,0:T(8,128)S(1)} %get-tuple-element.16), channel_id=1, source_target_pairs={{0,33},{1,34},{2,35},{3,36},{4,37},{5,38},{6,39},{7,40},{8,41},{9,... | collective-permute-start | bytes 294920 | tf_op jit(solution)/shard_map/ppermute | solution.py:286
  24.7 0.7 collective-permute-start
  26.0 1.4 %collective-permute-start.3 = (f32[192,128]{1,0:T(8,128)S(1)}, f32[192,128]{1,0:T(8,128)S(1)}, u32[]{:S(2)}, u32[]{:S(2)}) collective-permute-start(f32[192,128]{1,0:T(8,128)S(1)} %get-tuple-element.18), channel_id=1, source_target_pairs={{32,65},{33,66},{34,67},{35,68},{36,69},{37,70},{38,71},{39,72},{4... | collective-permute-start | bytes 294920 | tf_op jit(solution)/shard_map/ppermute | solution.py:286
  26.6 0.7 collective-permute-start.2
  27.9 1.4 %collective-permute-start.5 = (f32[192,128]{1,0:T(8,128)S(1)}, f32[192,128]{1,0:T(8,128)S(1)}, u32[]{:S(2)}, u32[]{:S(2)}) collective-permute-start(f32[192,128]{1,0:T(8,128)S(1)} %get-tuple-element.20), channel_id=1, source_target_pairs={{64,97},{65,98},{66,99},{67,100},{68,101},{69,102},{70,103},{71,10... | collective-permute-start | bytes 294920 | tf_op jit(solution)/shard_map/ppermute | solution.py:286
  28.6 0.7 collective-permute-start.4
  29.8 1.5 %collective-permute-start.7 = (f32[192,128]{1,0:T(8,128)S(1)}, f32[192,128]{1,0:T(8,128)S(1)}, u32[]{:S(2)}, u32[]{:S(2)}) collective-permute-start(f32[192,128]{1,0:T(8,128)S(1)} %get-tuple-element.22), channel_id=1, source_target_pairs={{96,129},{97,130},{98,131},{99,132},{100,133},{101,134},{102,135},... | collective-permute-start | bytes 294920 | tf_op jit(solution)/shard_map/ppermute | solution.py:286
  30.5 0.9 collective-permute-start.6
  31.9 1.4 %collective-permute-start.9 = (f32[192,128]{1,0:T(8,128)S(1)}, f32[192,128]{1,0:T(8,128)S(1)}, u32[]{:S(2)}, u32[]{:S(2)}) collective-permute-start(f32[192,128]{1,0:T(8,128)S(1)} %get-tuple-element.24), channel_id=1, source_target_pairs={{128,161},{129,162},{130,163},{131,164},{132,165},{133,166},{134,1... | collective-permute-start | bytes 294920 | tf_op jit(solution)/shard_map/ppermute | solution.py:286
  32.6 0.7 collective-permute-start.8
  33.9 1.4 %collective-permute-start.11 = (f32[192,128]{1,0:T(8,128)S(1)}, f32[192,128]{1,0:T(8,128)S(1)}, u32[]{:S(2)}, u32[]{:S(2)}) collective-permute-start(f32[192,128]{1,0:T(8,128)S(1)} %get-tuple-element.26), channel_id=1, source_target_pairs={{160,193},{161,194},{162,195},{163,196},{164,197},{165,198},{166,1... | collective-permute-start | bytes 294920 | tf_op jit(solution)/shard_map/ppermute | solution.py:286
  34.5 0.7 collective-permute-start.10
  35.8 2.0 %collective-permute-start.13 = (f32[192,128]{1,0:T(8,128)S(1)}, f32[192,128]{1,0:T(8,128)S(1)}, u32[]{:S(2)}, u32[]{:S(2)}) collective-permute-start(f32[192,128]{1,0:T(8,128)S(1)} %get-tuple-element.28), channel_id=1, source_target_pairs={{192,225},{193,226},{194,227},{195,228},{196,229},{197,230},{198,2... | collective-permute-start | bytes 294920 | tf_op jit(solution)/shard_map/ppermute | solution.py:286
  36.5 47.2 %collective-permute-start.12 = (f32[192,128]{1,0:T(8,128)S(1)}, f32[192,128]{1,0:T(8,128)S(1)}, u32[]{:S(2)}, u32[]{:S(2)}) collective-permute-start(f32[192,128]{1,0:T(8,128)S(1)} %get-tuple-element.28), channel_id=1, source_target_pairs={{192,224},{193,225},{194,226},{195,227},{196,228},{197,229},{198,2... | collective-permute-start | bytes 294920 | tf_op jit(solution)/shard_map/ppermute | solution.py:285

commit v5 on v4

--- a/solution.py
+++ b/solution.py
@@ -7,6 +7,7 @@
 from jax.experimental import pallas as pl
 from jax.experimental.pallas import tpu as pltpu
 from jax.sharding import PartitionSpec as P
+
 
 SB = 128
 PANEL = 8
@@ -16,6 +17,7 @@
 NT = (((1,), (1,)), ((), ()))
 TN = (((0,), (0,)), ((), ()))
 VMEM_BYTES = 24 * 1024 * 1024
+TURNS = 380
 VMEM_SPEC = pl.BlockSpec(memory_space=pltpu.VMEM)
 SMEM_SPEC = pl.BlockSpec(memory_space=pltpu.SMEM)
 
@@ -249,12 +251,27 @@
         out_ref[:, 32 + 4 * s : 36 + 4 * s, :] = factor[s].reshape(32, 4, SB)
 
 
+def hold_kernel(odd_ref, out_ref):
+    def turn(_, value):
+        return lax.rem(value * 5 + 3, 8191)
+
+    last = lax.fori_loop(0, odd_ref[0] * TURNS, turn, odd_ref[0])
+    out_ref[0] = jnp.where(last < 0, 1, 0)
+
+
 def shards(mps_cores, live_sizes, retained_sizes, pattern):
     n_site = lax.axis_size("site")
     n_row = lax.axis_size("row")
     site_at = lax.axis_index("site")
     row_at = lax.axis_index("row")
     sent = mps_cores.reshape(n_row, 32, SB)
+    held = pl.pallas_call(
+        hold_kernel,
+        out_shape=jax.ShapeDtypeStruct((1,), jnp.int32),
+        in_specs=[SMEM_SPEC],
+        out_specs=SMEM_SPEC,
+        name="hold",
+    )((site_at % 2).astype(jnp.int32).reshape(1))
     got = lax.all_to_all(sent, "row", split_axis=0, concat_axis=0, tiled=True)
     got = got.reshape(n_row, 2, 4, 4, SB)
     live, kept = live_sizes[0], retained_sizes[0]
@@ -265,7 +282,7 @@
     stacked = jnp.stack([cores[s, p] for s, p in ORDER])
     a_all = stacked.reshape(8 * SB, SB)
     at_all = jnp.swapaxes(stacked, 1, 2).reshape(8 * SB, SB)
-    head = jnp.stack([site_at, (site_at == 0).astype(jnp.int32), (row_at > 0).astype(jnp.int32)])
+    head = jnp.stack([site_at + held[0], (site_at == 0).astype(jnp.int32), (row_at > 0).astype(jnp.int32)])
     flags = jnp.concatenate([head.astype(jnp.int32), live, kept])
     params = pltpu.CompilerParams(vmem_limit_bytes=VMEM_BYTES)
     packet = jax.ShapeDtypeStruct(PACKET, F32)

time: 122 us -> 122 us (level)
  waiting for transfers between devices: 55.8 us -> 51 us
  Pallas kernels: 8.73 us -> 12.8 us
    all_to_all x1, waiting for transfers between devices: 9.86 us -> 5.08 us  [shards(): got = lax.all_to_all(sent, 'row', split_axis=0, concat_axis=0, tiled=True)]
    pallas_call x0 -> x1, Pallas kernels: none -> 4.12 us  [shards(): pl.pallas_call(hold_kernel, out_shape=jax.ShapeDtypeStruct((1,), jnp.int3...]
  transfers between devices with their start and end apart: 15 -> 15, of which waited for: 2 -> 2; matrix products, arithmetic and copies ran while one was open for 0% -> 0% of each run, Pallas kernels for 0% -> 3%
where the time goes in v5:
time: 122 us; the launch traced here: 121 us
  waiting for transfers between devices  51 us (42%)
  blocking collectives  31.2 us (26%)
  starting transfers between devices  21.2 us (17%)
  Pallas kernels  12.8 us (10%)
  local copies, waits for them, and re-layouts  3.24 us (3%)
  between operations  1.68 us (1%)
    ppermute x7, waiting for transfers between devices, shards(): lax.ppermute(factor, ('site', 'row'), [(here + i, there + i) for i in ran...  45.9 us
    all_to_all x1, blocking collectives, shards(): back = lax.all_to_all(out, 'row', split_axis=0, concat_axis=0, tiled=True)  31.2 us
    all_to_all x1, starting transfers between devices, shards(): got = lax.all_to_all(sent, 'row', split_axis=0, concat_axis=0, tiled=True)  11 us
    ppermute x7, starting transfers between devices, shards(): lax.ppermute(factor, ('site', 'row'), [(here + i, there + i) for i in ran...  5.29 us
    all_to_all x1, waiting for transfers between devices, shards(): got = lax.all_to_all(sent, 'row', split_axis=0, concat_axis=0, tiled=True)  5.08 us
    pallas_call x1, Pallas kernels, shards(): pl.pallas_call(functools.partial(last_kernel, n_site - 1), out_shape=jax....  4.87 us
    ppermute x7, starting transfers between devices, shards(): lax.ppermute(factor, ('site', 'row'), [(here + i, there + i + 1) for i in...  4.85 us
    pallas_call x1, Pallas kernels, shards(): pl.pallas_call(hold_kernel, out_shape=jax.ShapeDtypeStruct((1,), jnp.int3...  4.12 us
  transfers between devices with their start and end apart: 15, of which 2 were waited for; matrix products, arithmetic and copies ran while one was open for 0% of the time, Pallas kernels for 3%

profile of v5, /device:TPU:25, one launch (start us, length us, event | category | flops | bytes accessed | tf_op | source)
XLA Modules:
  0.0 121.3 jit_solution(10993279653752225658)
XLA Ops:
  0.6 11.0 %all-to-all-start = ((bf16[32,32,128]{2,1,0:T(8,128)(2,1)}), bf16[32,32,128]{2,1,0:T(8,128)(2,1)S(1)}, u32[]{:S(2)}, u32[]{:S(2)}) async-start(bf16[32,32,128]{2,1,0:T(8,128)(2,1)} %bitcast.64), calls=%async_computation | async-start | bytes 524288 | tf_op jit(solution)/shard_map/all_to_all | solution.py:275
  11.7 4.1 %hold.1 = s32[1]{0:T(128)} custom-call(s32[1]{0:T(128)} %bitcast.odd_ref), custom_call_target="tpu_custom_call" | custom-call | tf_op jit(solution)/shard_map/hold/pallas_call | solution.py:268
  16.5 0.0 copy-start
  16.5 0.0 copy-start.1
  16.5 0.6 copy-done
  17.1 0.0 copy-done.1
  17.2 0.1 concatenate.3.flags
  17.2 0.6 copy-done.2
  17.8 0.1 fusion.8
  17.9 5.1 %all-to-all-done = bf16[32,32,128]{2,1,0:T(8,128)(2,1)S(1)} async-done(((bf16[32,32,128]{2,1,0:T(8,128)(2,1)}), bf16[32,32,128]{2,1,0:T(8,128)(2,1)S(1)}, u32[]{:S(2)}, u32[]{:S(2)}) %all-to-all-start) | async-done | bytes 262176 | tf_op jit(solution)/shard_map/all_to_all | solution.py:275
  23.0 0.1 copy.13
  23.2 0.2 copy.14
  23.5 0.6 round.7
  24.0 0.7 collective-permute-start.1
  24.7 0.7 collective-permute-start
  25.4 0.0 collective-permute-done.1.low_ref
  25.4 0.0 collective-permute-done.own_ref
  25.4 0.6 round.8
  26.0 0.7 collective-permute-start.3
  26.6 0.7 collective-permute-start.2
  27.3 0.0 collective-permute-done.3.low_ref
  27.3 0.0 collective-permute-done.2.own_ref
  27.3 0.6 round.9
  27.9 0.7 collective-permute-start.5
  28.6 0.7 collective-permute-start.4
  29.2 0.0 collective-permute-done.5.low_ref
  29.2 0.0 collective-permute-done.4.own_ref
  29.3 0.6 round.10
  29.8 0.8 collective-permute-start.7
  30.7 0.7 collective-permute-start.6
  31.4 0.0 collective-permute-done.6.own_ref
  31.4 0.6 round.11
  31.9 0.7 collective-permute-start.9
  32.6 0.7 collective-permute-start.8
  33.3 0.0 collective-permute-done.9.low_ref
  33.3 0.0 collective-permute-done.8.own_ref
  33.3 0.6 round.12
  33.9 0.7 collective-permute-start.11
  34.5 0.7 collective-permute-start.10
  35.2 0.0 collective-permute-done.11.low_ref
  35.2 0.6 round.13
  35.8 0.7 collective-permute-start.13
  36.5 1.3 %collective-permute-start.12 = (f32[192,128]{1,0:T(8,128)S(1)}, f32[192,128]{1,0:T(8,128)S(1)}, u32[]{:S(2)}, u32[]{:S(2)}) collective-permute-start(f32[192,128]{1,0:T(8,128)S(1)} %get-tuple-element.28), channel_id=1, source_target_pairs={{192,224},{193,225},{194,226},{195,227},{196,228},{197,229},{198,2... | collective-permute-start | bytes 294920 | tf_op jit(solution)/shard_map/ppermute | solution.py:302
  37.8 45.9 %collective-permute-done.12.own_ref = f32[192,128]{1,0:T(8,128)S(1)} collective-permute-done((f32[192,128]{1,0:T(8,128)S(1)}, f32[192,128]{1,0:T(8,128)S(1)}, u32[]{:S(2)}, u32[]{:S(2)}) %collective-permute-start.12) | collective-permute-done | bytes 98336 | tf_op jit(solution)/shard_map/ppermute | solution.py:302
  83.7 4.9 %last.1 = f32[32,40,128]{2,1,0:T(8,128)S(1)} custom-call(s32[7]{0:T(128)S(1)} %concatenate.3.flags, f32[192,128]{1,0:T(8,128)S(1)} %collective-permute-done.12.own_ref, f32[192,128]{1,0:T(8,128)S(1)} %collective-permute-done.13.low_ref, f32[2,192,128]{2,1,0:T(8,128)S(1)} %get-tuple-element.29.state_ref, bf16[1024,128]{1,0:T(8,128)(2,1)S(1)} %bitcast.58, ...), custom_call_target="tpu_custom_call" | custom-call | tf_op jit(solution)/shard_map/last/pallas_call | solution.py:304
  88.6 31.2 %all_to_all.10 = f32[32,40,128]{2,1,0:T(8,128)S(1)} all-to-all(f32[32,40,128]{2,1,0:T(8,128)S(1)} %last.1), channel_id=1, replica_groups=mesh['site'=8,'row'=32] {'row'}, dimensions={0} | all-to-all | bytes 1310720 | tf_op jit(solution)/shard_map/all_to_all | solution.py:313
  119.7 0.7 slice.49
  120.4 0.9 slice.48
  (16 shorter events, 0.1 us)
Async XLA Ops:
  0.6 22.4 %all-to-all-start = ((bf16[32,32,128]{2,1,0:T(8,128)(2,1)}), bf16[32,32,128]{2,1,0:T(8,128)(2,1)S(1)}, u32[]{:S(2)}, u32[]{:S(2)}) async-start(bf16[32,32,128]{2,1,0:T(8,128)(2,1)} %bitcast.64), calls=%async_computation | async-start | bytes 524288 | tf_op jit(solution)/shard_map/all_to_all | solution.py:275
  16.5 0.7 copy-start
  16.5 0.7 copy-start.1
  17.2 0.7 copy-start.2
  24.0 1.4 %collective-permute-start.1 = (f32[192,128]{1,0:T(8,128)S(1)}, f32[192,128]{1,0:T(8,128)S(1)}, u32[]{:S(2)}, u32[]{:S(2)}) collective-permute-start(f32[192,128]{1,0:T(8,128)S(1)} %get-tuple-element.16), channel_id=1, source_target_pairs={{0,33},{1,34},{2,35},{3,36},{4,37},{5,38},{6,39},{7,40},{8,41},{9,... | collective-permute-start | bytes 294920 | tf_op jit(solution)/shard_map/ppermute | solution.py:303
  24.7 0.7 collective-permute-start
  26.0 1.4 %collective-permute-start.3 = (f32[192,128]{1,0:T(8,128)S(1)}, f32[192,128]{1,0:T(8,128)S(1)}, u32[]{:S(2)}, u32[]{:S(2)}) collective-permute-start(f32[192,128]{1,0:T(8,128)S(1)} %get-tuple-element.18), channel_id=1, source_target_pairs={{32,65},{33,66},{34,67},{35,68},{36,69},{37,70},{38,71},{39,72},{4... | collective-permute-start | bytes 294920 | tf_op jit(solution)/shard_map/ppermute | solution.py:303
  26.6 0.7 collective-permute-start.2
  27.9 1.4 %collective-permute-start.5 = (f32[192,128]{1,0:T(8,128)S(1)}, f32[192,128]{1,0:T(8,128)S(1)}, u32[]{:S(2)}, u32[]{:S(2)}) collective-permute-start(f32[192,128]{1,0:T(8,128)S(1)} %get-tuple-element.20), channel_id=1, source_target_pairs={{64,97},{65,98},{66,99},{67,100},{68,101},{69,102},{70,103},{71,10... | collective-permute-start | bytes 294920 | tf_op jit(solution)/shard_map/ppermute | solution.py:303
  28.6 0.7 collective-permute-start.4
  29.8 1.5 %collective-permute-start.7 = (f32[192,128]{1,0:T(8,128)S(1)}, f32[192,128]{1,0:T(8,128)S(1)}, u32[]{:S(2)}, u32[]{:S(2)}) collective-permute-start(f32[192,128]{1,0:T(8,128)S(1)} %get-tuple-element.22), channel_id=1, source_target_pairs={{96,129},{97,130},{98,131},{99,132},{100,133},{101,134},{102,135},... | collective-permute-start | bytes 294920 | tf_op jit(solution)/shard_map/ppermute | solution.py:303
  30.7 0.7 collective-permute-start.6
  31.9 1.4 %collective-permute-start.9 = (f32[192,128]{1,0:T(8,128)S(1)}, f32[192,128]{1,0:T(8,128)S(1)}, u32[]{:S(2)}, u32[]{:S(2)}) collective-permute-start(f32[192,128]{1,0:T(8,128)S(1)} %get-tuple-element.24), channel_id=1, source_target_pairs={{128,161},{129,162},{130,163},{131,164},{132,165},{133,166},{134,1... | collective-permute-start | bytes 294920 | tf_op jit(solution)/shard_map/ppermute | solution.py:303
  32.6 0.7 collective-permute-start.8
  33.9 1.4 %collective-permute-start.11 = (f32[192,128]{1,0:T(8,128)S(1)}, f32[192,128]{1,0:T(8,128)S(1)}, u32[]{:S(2)}, u32[]{:S(2)}) collective-permute-start(f32[192,128]{1,0:T(8,128)S(1)} %get-tuple-element.26), channel_id=1, source_target_pairs={{160,193},{161,194},{162,195},{163,196},{164,197},{165,198},{166,1... | collective-permute-start | bytes 294920 | tf_op jit(solution)/shard_map/ppermute | solution.py:303
  34.5 0.7 collective-permute-start.10
  35.8 2.0 %collective-permute-start.13 = (f32[192,128]{1,0:T(8,128)S(1)}, f32[192,128]{1,0:T(8,128)S(1)}, u32[]{:S(2)}, u32[]{:S(2)}) collective-permute-start(f32[192,128]{1,0:T(8,128)S(1)} %get-tuple-element.28), channel_id=1, source_target_pairs={{192,225},{193,226},{194,227},{195,228},{196,229},{197,230},{198,2... | collective-permute-start | bytes 294920 | tf_op jit(solution)/shard_map/ppermute | solution.py:303
  36.5 47.2 %collective-permute-start.12 = (f32[192,128]{1,0:T(8,128)S(1)}, f32[192,128]{1,0:T(8,128)S(1)}, u32[]{:S(2)}, u32[]{:S(2)}) collective-permute-start(f32[192,128]{1,0:T(8,128)S(1)} %get-tuple-element.28), channel_id=1, source_target_pairs={{192,224},{193,225},{194,226},{195,227},{196,228},{197,229},{198,2... | collective-permute-start | bytes 294920 | tf_op jit(solution)/shard_map/ppermute | solution.py:302
